TPU v7x, 32 devices: a whole 2x2x4 slice. The times are simulated.
32 devices in a mesh: seq: 4 (over y, x), fsdp: 8 (over z, core).
Axes of the slice: x: 2, y: 2, z: 4, core: 2. Of those that a mesh axis runs over, the one named last changes fastest.
Arguments:
- hidden_in: bfloat16 [8, 1024, 1024], P('fsdp', 'seq'), may hold values from -10 to 10
- segment_ids: int32 [8, 1024], P('fsdp'), may hold values from 0 to 2, never falling along the last dimension, each value on 1 to 768 neighbouring positions
- valid_tokens: int32 [8, 1024], P('fsdp'), may hold values from 0 to 1
- w_qkv: bfloat16 [1024, 3072], P('fsdp'), may hold values from -0.1875 to 0.1875
- w_attn_out: bfloat16 [1024, 1024], P('fsdp'), may hold values from -2 to 2
- w_in_proj: bfloat16 [1024, 5248], P('fsdp'), may hold values from -0.1875 to 0.1875
- w_out_proj: bfloat16 [2624, 1024], P('fsdp'), may hold values from -0.125 to 0.125
- attn_gain: bfloat16 [1024], P('fsdp'), may hold values from 0.25 to 1.75
- mlp_gain: bfloat16 [1024], P('fsdp'), may hold values from 0.25 to 1.75
- cotangent: bfloat16 [8, 1024, 1024], P('fsdp', 'seq'), may hold values from -6 to 6
Outputs:
- hidden_out: bfloat16 [8, 1024, 1024], P('fsdp', 'seq')
- grad_in: float32 [8, 1024, 1024], P('fsdp', 'seq')
- grad_qkv: float32 [1024, 3072], P('fsdp')
- grad_attn_out: float32 [1024, 1024], P('fsdp')
- grad_in_proj: float32 [1024, 5248], P('fsdp')
- grad_out_proj: float32 [2624, 1024], P('fsdp')
- grad_attn_gain: float32 [1024], P('fsdp')
- grad_mlp_gain: float32 [1024], P('fsdp')
- rms_values: float32 [3], replicated
All inputs are finite; a program needn't handle non-finite values.
Results may differ from a plain program's by a relative error of at most 0.014.
The roundings to bfloat16 on the way count: a program that leaves them out, or rounds other values in their place, can miss the bound.
Values may be sent and summed in bfloat16 or wider, within the bound.
No kernel may reach another device: no remote copies, remote signals or barrier semaphores. Data moves between devices by JAX's collectives and lax.ppermute only.
A program may use at most 192 MiB of HBM per device.

v0:
```python
import functools

import jax
import jax.numpy as jnp
from jax import lax
from jax.experimental import pallas as pl
from jax.experimental.pallas import tpu as pltpu
from jax.sharding import PartitionSpec as P

D = 1024
HEADS = 16
HD = 64
FF = 2624

ROPE_BASE = 160000.0
NORM_EPS = 1e-05
LANES = 128
BF = jnp.bfloat16
F32 = jnp.float32


def swap(x, axis, bit):
    return lax.ppermute(x, axis, [(i, i ^ bit) for i in range(lax.axis_size(axis))])


def after(x, *others):
    return lax.optimization_barrier((x, others))[0]


def share_seq(block):
    return [block] + [swap(block, "seq", k) for k in range(1, lax.axis_size("seq"))]


def relay_first(block):
    return swap(block, "seq", 1), swap(block, "seq", 2)


def relay_last(block, one, two):
    if lax.axis_size("seq") != 4:
        return share_seq(block)
    half = block.shape[0] // 2
    upper, lower = swap(two[:half], "seq", 1), swap(one[half:], "seq", 2)
    return [block, one, two, jnp.concatenate([upper, lower], axis=0)]


def exchange_seq(blocks):
    return lax.all_to_all(blocks, "seq", split_axis=0, concat_axis=0, tiled=True)


def sum_blocks(blocks):
    rows = blocks.shape[0] // lax.axis_size("seq")
    total = blocks[:rows].astype(F32)
    for i in range(1, lax.axis_size("seq")):
        total = total + blocks[i * rows : (i + 1) * rows].astype(F32)
    return total


def paired():
    return lax.axis_size("fsdp") == 2 * lax.axis_size("seq")


def gather_rows(block):
    return lax.all_gather(block, "fsdp", axis=0, tiled=True)


def transpose_devices(x):
    seq, fsdp = lax.axis_size("seq"), lax.axis_size("fsdp")
    pairs = [
        (s * fsdp + 2 * z + c, z * fsdp + 2 * s + c)
        for s in range(seq)
        for z in range(fsdp // 2)
        for c in range(2)
    ]
    return lax.ppermute(x, ("seq", "fsdp"), pairs)


def tree_sum(values):
    while len(values) > 1:
        values = [values[i] + values[i + 1] for i in range(0, len(values), 2)]
    return values[0]


def in_three(values):
    terms = []
    for _ in range(3):
        terms.append(lax.reduce_precision(values, 8, 7))
        values = values - terms[-1]
    return jnp.stack(terms).astype(BF)


def from_three(terms):
    terms = terms.astype(F32)
    return (terms[0] + terms[1]) + terms[2]


def half_swap(values):
    width = values.shape[1]
    lane = lax.broadcasted_iota(jnp.int32, values.shape, 1)
    ahead = pltpu.roll(values, width - HD // 2, 1)
    behind = pltpu.roll(values, HD // 2, 1)
    return jnp.where(lane % HD < HD // 2, ahead, behind)


def wide(table, width):
    return jnp.concatenate([table] * (width // table.shape[1]), axis=1)


def qkv_kernel(*refs):
    count = 4
    xs = refs[:count]
    w_ref, gain_ref, cos_ref, sin_ref, a_ref, q_ref, k_ref, v_ref, held = refs[count:]
    step = pl.program_id(0)
    for i in range(count):

        @pl.when(step == i)
        def _():
            held[...] = xs[i][...].astype(F32)

    values = held[...]
    centered = values - jnp.mean(values, axis=1, keepdims=True)
    variance = jnp.mean(centered * centered, axis=1, keepdims=True)
    low = (centered * lax.rsqrt(variance + NORM_EPS) * gain_ref[...]).astype(BF)
    a_ref[...] = low
    p = jnp.dot(low, w_ref[...], preferred_element_type=F32)
    part = p.shape[1] // 3
    turned = p[:, : 2 * part]
    turned = turned * wide(cos_ref[...], 2 * part) + half_swap(turned) * wide(sin_ref[...], 2 * part)
    q_ref[...] = turned[:, :part].astype(BF) * (HD**-0.5)
    k_ref[...] = turned[:, part:].astype(BF)
    v_ref[...] = p[:, 2 * part :].astype(BF)


def project_qkv(blocks, weight, gain, cosine, sine):
    rows, width = blocks[0].shape
    part = (weight.shape[1] - LANES) // 4
    count = len(blocks)
    whole = lambda a: pl.BlockSpec(a.shape, lambda i: (0, 0))
    tile = lambda n: pl.BlockSpec((rows, n), lambda i: (i, 0))
    shape = lambda n: jax.ShapeDtypeStruct((rows * count, n), BF)
    return pl.pallas_call(
        qkv_kernel,
        grid=(count,),
        in_specs=[whole(b) for b in blocks]
        + [pl.BlockSpec((width, 3 * part), lambda i: (0, 0)), whole(gain), tile(cosine.shape[1]), tile(sine.shape[1])],
        out_specs=[tile(width), tile(part), tile(part), tile(part)],
        out_shape=[shape(width), shape(part), shape(part), shape(part)],
        scratch_shapes=[pltpu.VMEM((rows, width), F32)],
        cost_estimate=pl.CostEstimate(
            flops=2 * rows * count * width * 3 * part,
            bytes_accessed=2 * rows * count * (2 * width + 3 * part) + 2 * width * 3 * part,
            transcendentals=0,
        ),
        name="qkv",
    )(*blocks, weight, gain, cosine, sine)


def mask_bias(seg_col, valid_col, seg_row, first_row):
    shape = (seg_col.shape[0], seg_row.shape[1])
    key = lax.broadcasted_iota(jnp.int32, shape, 0)
    query = lax.broadcasted_iota(jnp.int32, shape, 1) + first_row
    allowed = (seg_col == seg_row) & ((valid_col > 0) | (key == query))
    return jnp.where(allowed, 0.0, -1e30)


def forward_kernel(q_ref, k_ref, v_ref, segc_ref, valc_ref, segr_ref, o_ref, lse_ref, vt_ref, ot_ref, bias_ref):
    step = pl.program_id(0)
    rows, width = q_ref.shape

    @pl.when(step == 0)
    def _():
        vt_ref[...] = v_ref[...].T

    bias_ref[...] = mask_bias(segc_ref[...], valc_ref[...], segr_ref[...], step * rows)
    qt = q_ref[...].T
    feature = lax.broadcasted_iota(jnp.int32, qt.shape, 0) // HD

    def head(h, carry):
        mine = jnp.where(feature == h, qt, jnp.zeros_like(qt))
        scores = jnp.dot(k_ref[...], mine, preferred_element_type=F32) + bias_ref[...]
        top = jnp.max(scores, axis=0, keepdims=True)
        exponent = jnp.exp(scores - top)
        total = jnp.sum(exponent, axis=0, keepdims=True)
        weights = (exponent * (1.0 / total)).astype(BF)
        start = pl.multiple_of(h * HD, HD)
        ot_ref[pl.ds(start, HD), :] = jnp.dot(
            vt_ref[pl.ds(start, HD), :], weights, preferred_element_type=F32
        )
        lse_ref[pl.ds(h, 1), :] = top + jnp.log(total)
        return carry

    lax.fori_loop(0, width // HD, head, 0)
    o_ref[...] = ot_ref[...].T.astype(BF)


def attend_forward(q, k, v, seg_col, valid_col, seg_row, rows):
    length, width = q.shape
    whole = lambda a: pl.BlockSpec(a.shape, lambda i: (0, 0))
    tile = pl.BlockSpec((rows, width), lambda i: (i, 0))
    return pl.pallas_call(
        forward_kernel,
        grid=(length // rows,),
        in_specs=[tile, whole(k), whole(v), whole(seg_col), whole(valid_col), pl.BlockSpec((1, rows), lambda i: (0, i))],
        out_specs=[tile, pl.BlockSpec((8, rows), lambda i: (0, i))],
        out_shape=[jax.ShapeDtypeStruct((length, width), BF), jax.ShapeDtypeStruct((8, length), F32)],
        scratch_shapes=[pltpu.VMEM((width, length), BF), pltpu.VMEM((width, rows), F32), pltpu.VMEM((length, rows), F32)],
        cost_estimate=pl.CostEstimate(
            flops=4 * length * length * width, bytes_accessed=8 * length * width, transcendentals=length * length * 4
        ),
        name="attend",
    )(q, k, v, seg_col, valid_col, seg_row)


def backward_kernel(
    q_ref, go_ref, lse_ref, k_ref, v_ref, segc_ref, valc_ref, segr_ref, cos_ref, sin_ref,
    gp_ref, kt_ref, dk_ref, dv_ref, dqt_ref, bias_ref,
):
    step = pl.program_id(0)
    rows, width = q_ref.shape

    @pl.when(step == 0)
    def _():
        kt_ref[...] = k_ref[...].T
        dk_ref[...] = jnp.zeros_like(dk_ref)
        dv_ref[...] = jnp.zeros_like(dv_ref)

    bias_ref[...] = mask_bias(segc_ref[...], valc_ref[...], segr_ref[...], step * rows)
    qt, got = q_ref[...].T, go_ref[...].T
    feature = lax.broadcasted_iota(jnp.int32, qt.shape, 0) // HD
    lane = lax.broadcasted_iota(jnp.int32, (rows, width), 1) // HD
    none = jnp.zeros_like(qt)
    none_row = jnp.zeros((rows, width), BF)

    def head(h, carry):
        scores = jnp.dot(k_ref[...], jnp.where(feature == h, qt, none), preferred_element_type=F32)
        weights = jnp.exp(scores + bias_ref[...] - lse_ref[pl.ds(h, 1), :])
        upstream = jnp.dot(v_ref[...], jnp.where(feature == h, got, none), preferred_element_type=F32)
        inner = jnp.sum(weights * upstream, axis=0, keepdims=True)
        low = (weights * (upstream - inner)).astype(BF)
        dv_ref[...] += jnp.dot(
            weights.astype(BF), jnp.where(lane == h, go_ref[...], none_row), preferred_element_type=F32
        )
        dk_ref[...] += jnp.dot(low, jnp.where(lane == h, q_ref[...], none_row), preferred_element_type=F32)
        start = pl.multiple_of(h * HD, HD)
        dqt_ref[pl.ds(start, HD), :] = jnp.dot(kt_ref[pl.ds(start, HD), :], low, preferred_element_type=F32)
        return carry

    lax.fori_loop(0, width // HD, head, 0)

    def unturn(values, cosine, sine):
        values = values.astype(BF).astype(F32)
        return (values * wide(cosine, width) - half_swap(values) * wide(sine, width)).astype(BF)

    here = pl.ds(pl.multiple_of(step * rows, rows), rows)
    gp_ref[here, :width] = unturn(dqt_ref[...].T * (HD**-0.5), cos_ref[here, :], sin_ref[here, :])

    @pl.when(step == pl.num_programs(0) - 1)
    def _():
        gp_ref[:, width : 2 * width] = unturn(dk_ref[...], cos_ref[...], sin_ref[...])
        gp_ref[:, 2 * width :] = dv_ref[...].astype(BF)


def attend_backward(q, k, v, grad_out, lse, seg_col, valid_col, seg_row, cosine, sine, rows):
    length, width = q.shape
    whole = lambda a: pl.BlockSpec(a.shape, lambda i: (0, 0))
    tile = pl.BlockSpec((rows, width), lambda i: (i, 0))
    return pl.pallas_call(
        backward_kernel,
        grid=(length // rows,),
        in_specs=[
            tile, tile, pl.BlockSpec((8, rows), lambda i: (0, i)), whole(k), whole(v),
            whole(seg_col), whole(valid_col), pl.BlockSpec((1, rows), lambda i: (0, i)), whole(cosine), whole(sine),
        ],
        out_specs=pl.BlockSpec((length, 3 * width), lambda i: (0, 0)),
        out_shape=jax.ShapeDtypeStruct((length, 3 * width), BF),
        scratch_shapes=[
            pltpu.VMEM((width, length), BF), pltpu.VMEM((length, width), F32), pltpu.VMEM((length, width), F32),
            pltpu.VMEM((width, rows), F32), pltpu.VMEM((length, rows), F32),
        ],
        cost_estimate=pl.CostEstimate(
            flops=10 * length * length * width, bytes_accessed=20 * length * width, transcendentals=length * length * 4
        ),
        name="attend_back",
    )(q, grad_out, lse, k, v, seg_col, valid_col, seg_row, cosine, sine)


def erf(x):
    x = jnp.clip(x, -3.832506856900711, 3.832506856900711)
    square = x * x
    top = 0.00022905065861350646
    for c in (0.0034082910107109506, 0.050955695062380861, 0.18520832239976145, 1.128379143519084):
        top = top * square + c
    low = -1.1791602954361697e-7
    for c in (0.000023547966471313185, 0.0010179625278914885, 0.014070470171167667, 0.11098505178285362, 0.49746925110067538, 1.0):
        low = low * square + c
    return x * top / low


def nt(a, b):
    return lax.dot_general(a, b, (((1,), (1,)), ((), ())), preferred_element_type=F32)


def feed_kernel(hidden, me_ref, b_ref, g_ref, w_ref, *refs):
    m_ref, gi_ref, gg_ref, gb_ref, mlp_ref = refs[-5:]
    b = b_ref[...]
    slot = w_ref.shape[1] // 3
    wi_ref, wg_ref, wd_ref = (w_ref.at[:, i * slot : i * slot + hidden] for i in range(3))
    inner = jnp.dot(b, wi_ref[...], preferred_element_type=F32)
    gate = jnp.dot(b, wg_ref[...], preferred_element_type=F32)
    upstream = jnp.dot(g_ref[...], wd_ref[...], preferred_element_type=F32)
    half = 0.5 * (1.0 + erf(inner * 0.7071067811865476))
    gelu = inner * half
    slope = half + inner * jnp.exp(-0.5 * inner * inner) * 0.3989422804014327
    m = (gelu * gate).astype(BF)
    gi = (upstream * gate * slope).astype(BF)
    gg = (upstream * gelu).astype(BF)
    m_ref[...] = m
    gi_ref[...] = gi
    gg_ref[...] = gg
    gb_ref[...] = (nt(gi, wi_ref[...]) + nt(gg, wg_ref[...])).astype(gb_ref.dtype)
    mlp_ref[...] = nt(m, wd_ref[...]).astype(mlp_ref.dtype)


def feed_forward(b, g, w, hidden, me, place, count, dtype, onto):
    rows, width = b.shape
    whole = lambda r, n: pl.BlockSpec((r, n), lambda i, me: (0, 0))
    narrow = jax.ShapeDtypeStruct((rows, hidden), BF)
    operands, specs = [b, g, w], [whole(rows, width), whole(rows, width), whole(*w.shape)]
    if onto is not None:
        operands.append(onto)
        specs.append(pl.BlockSpec(memory_space=pl.ANY))
    return pl.pallas_call(
        functools.partial(feed_kernel, hidden),
        grid_spec=pltpu.PrefetchScalarGridSpec(
            num_scalar_prefetch=1,
            grid=(1,),
            in_specs=specs,
            out_specs=[whole(rows, hidden)] * 3
            + [whole(rows, width), pl.BlockSpec((rows, width), lambda i, me: (me[0] ^ place, 0))],
        ),
        out_shape=[narrow] * 3
        + [jax.ShapeDtypeStruct((rows, width), dtype), jax.ShapeDtypeStruct((rows * count, width), BF)],
        input_output_aliases={} if onto is None else {4: 4},
        cost_estimate=pl.CostEstimate(
            flops=12 * rows * width * hidden,
            bytes_accessed=6 * width * hidden + 8 * rows * width + 6 * rows * hidden,
            transcendentals=rows * hidden,
        ),
        name="feed",
    )(me[None], *operands)


def tn(a, b):
    return lax.dot_general(a, b, (((0,), (0,)), ((), ())), preferred_element_type=F32)


def weight_kernel(count, slot, pairs, *refs):
    out_ref = refs[-1]
    hidden = refs[(pairs[0][1]) * count].shape[1]
    for place, (left, right) in enumerate(pairs):
        total = None
        for i in range(count):
            term = tn(refs[left * count + i][...], refs[right * count + i][...])
            total = term if total is None else total + term
        out_ref[:, place * slot : place * slot + hidden] = total.astype(BF)
        if hidden < slot:
            out_ref[:, place * slot + hidden : (place + 1) * slot] = jnp.zeros((out_ref.shape[0], slot - hidden), BF)


def weight_gradients(lefts, rights, pairs, slots, place, onto=None):
    count = len(lefts[0])
    rows, width = lefts[0][0].shape
    hidden = rights[0][0].shape[1]
    slot = -(-hidden // LANES) * LANES
    wide_spec = pl.BlockSpec((rows, 256), lambda i: (0, i))
    whole = pl.BlockSpec((rows, hidden), lambda i: (0, 0))
    operands = [b for group in lefts for b in group] + [b for group in rights for b in group]
    specs = [wide_spec] * (len(lefts) * count) + [whole] * (len(rights) * count)
    aliases = {}
    if onto is not None:
        aliases = {len(operands): 0}
        operands.append(onto)
        specs.append(pl.BlockSpec(memory_space=pl.ANY))
    return pl.pallas_call(
        functools.partial(weight_kernel, count, slot, pairs),
        grid=(width // 256,),
        in_specs=specs,
        out_specs=pl.BlockSpec((256, len(pairs) * slot), lambda i: (i, place // len(pairs))),
        out_shape=jax.ShapeDtypeStruct((width, slots * slot), BF),
        input_output_aliases=aliases,
        cost_estimate=pl.CostEstimate(
            flops=2 * len(pairs) * rows * count * width * hidden,
            bytes_accessed=2 * count * rows * (len(lefts) * width + len(rights) * hidden),
            transcendentals=0,
        ),
        name="weight_gradients",
    )(*operands)


def last_kernel(me_ref, a_ref, gp_ref, mine_ref, away_ref):
    total = tn(a_ref[...], gp_ref[...])

    @pl.when(pl.program_id(0) % 2 == 0)
    def _():
        mine_ref[...] = total

    @pl.when(pl.program_id(0) % 2 == 1)
    def _():
        away_ref[...] = total.astype(BF)


def last_gradients(a, gp, me, size):
    length, width = a.shape
    rows, columns = width // size, gp.shape[1]
    out = lambda dtype: jax.ShapeDtypeStruct((width // 2, columns), dtype)
    return pl.pallas_call(
        last_kernel,
        grid_spec=pltpu.PrefetchScalarGridSpec(
            num_scalar_prefetch=1,
            grid=(size,),
            in_specs=[
                pl.BlockSpec((length, rows), lambda i, me: (0, me[0] ^ i)),
                pl.BlockSpec((length, columns), lambda i, me: (0, 0)),
            ],
            out_specs=[pl.BlockSpec((rows, columns), lambda i, me: (i // 2, 0))] * 2,
        ),
        out_shape=[out(F32), out(BF)],
        cost_estimate=pl.CostEstimate(
            flops=2 * length * width * columns,
            bytes_accessed=2 * length * (width + columns) + 3 * width * columns,
            transcendentals=0,
        ),
        name="last_gradients",
    )(me[None], a, gp)


def qkv_back_kernel(me_ref, gp_ref, w_ref, out_ref):
    out_ref[...] = nt(gp_ref[...], w_ref[...]).astype(BF)


def project_back(gp, weight, me, count):
    rows, width = gp.shape[0] // count, weight.shape[0]
    return pl.pallas_call(
        qkv_back_kernel,
        grid_spec=pltpu.PrefetchScalarGridSpec(
            num_scalar_prefetch=1,
            grid=(count,),
            in_specs=[
                pl.BlockSpec((rows, gp.shape[1]), lambda i, me: (i, 0)),
                pl.BlockSpec((width, gp.shape[1]), lambda i, me: (0, 0)),
            ],
            out_specs=pl.BlockSpec((rows, width), lambda i, me: (me[0] ^ i, 0)),
        ),
        out_shape=jax.ShapeDtypeStruct((rows * count, width), BF),
        cost_estimate=pl.CostEstimate(
            flops=2 * rows * count * width * gp.shape[1],
            bytes_accessed=2 * (rows * count * (width + gp.shape[1]) + width * gp.shape[1]),
            transcendentals=0,
        ),
        name="project_back",
    )(me[None], gp, weight)


def ordered(refs, me, piece):
    values = [ref[piece] for ref in refs]
    bit = 1
    while bit < len(values):
        flip = (me & bit) != 0
        values = [jnp.where(flip, values[k ^ bit], values[k]) for k in range(len(values))]
        bit *= 2
    return values


def gain_part(w_ref, grad_ref, gain_ref, out_ref):
    total = jnp.sum(w_ref[...].astype(F32) * grad_ref[...], axis=1, keepdims=True)
    total = jnp.broadcast_to(total, (total.shape[0], LANES)).T
    out_ref[...] = total[:1] / gain_ref[...].astype(F32)


def last_rows_kernel(count, me_ref, *refs):
    blocks, (w_ref, gain_ref, qkv_ref, out_ref, gg_ref) = refs[:count], refs[count:]
    part = (blocks[0].shape[1] - LANES) // (3 + count)
    piece = lambda i: (slice(None), slice(i * part, (i + 1) * part))
    for i in range(3):
        for j, value in enumerate(ordered(blocks, me_ref[0], piece(i))):
            first = (i * count + j) * part
            qkv_ref[:, first : first + part] = value.astype(F32)
    for j in range(count):
        total = None
        for value in ordered(blocks, me_ref[0], piece(3 + j)):
            total = value.astype(F32) if total is None else total + value.astype(F32)
        out_ref[:, j * part : (j + 1) * part] = total
    gain_part(w_ref, qkv_ref, gain_ref, gg_ref)


def in_rows_kernel(count, hidden, me_ref, *refs):
    blocks, (w_ref, gain_ref, in_ref, gg_ref) = refs[:count], refs[count:]
    slot = blocks[0].shape[1] // 2
    for i in range(2):
        piece = (slice(None), slice(i * slot, i * slot + hidden))
        values = [value.astype(F32) for value in ordered(blocks, me_ref[0], piece)]
        in_ref[:, i * count * hidden : (i + 1) * count * hidden] = jnp.concatenate(values, axis=1)
    gain_part(w_ref, in_ref, gain_ref, gg_ref)


def finish_rows(kernel, blocks, weight, gain, me, widths, name):
    rows = weight.shape[0]
    shapes = [jax.ShapeDtypeStruct((rows, n), F32) for n in widths] + [jax.ShapeDtypeStruct((1, rows), F32)]
    return pl.pallas_call(
        kernel,
        in_specs=[pl.BlockSpec(memory_space=pltpu.SMEM)] + [pl.BlockSpec(memory_space=pltpu.VMEM)] * (len(blocks) + 2),
        out_shape=shapes,
        cost_estimate=pl.CostEstimate(flops=0, bytes_accessed=8 * rows * sum(widths), transcendentals=0),
        name=name,
    )(me[None], *blocks, weight, gain[None])


def normal(values):
    centered = values - jnp.mean(values, axis=-1, keepdims=True)
    scale = lax.rsqrt(jnp.mean(centered * centered, axis=-1, keepdims=True) + NORM_EPS)
    return centered * scale, scale


def norm_back(upstream, gain, values):
    unit, scale = normal(values)
    weighted = upstream * gain
    return scale * (
        weighted
        - jnp.mean(weighted, axis=-1, keepdims=True)
        - unit * jnp.mean(weighted * unit, axis=-1, keepdims=True)
    )


def matmul(a, b):
    return jnp.dot(a, b, preferred_element_type=F32)


def matmul_nt(a, b):
    return lax.dot_general(a, b, (((1,), (1,)), ((), ())), preferred_element_type=F32)


def matmul_tn(a, b):
    return lax.dot_general(a, b, (((0,), (0,)), ((), ())), preferred_element_type=F32)


def on_device(
    hidden_in, segment_ids, valid_tokens, w_qkv, w_attn_out, w_in_proj, w_out_proj, attn_gain, mlp_gain, cotangent
):
    seq_size, fsdp_size = lax.axis_size("seq"), lax.axis_size("fsdp")
    seq, fsdp = lax.axis_index("seq"), lax.axis_index("fsdp")
    x_low, cot = hidden_in[0], cotangent[0]
    tokens = x_low.shape[0]
    length = tokens * seq_size
    part = D // seq_size
    hidden = FF // seq_size
    rel = [seq ^ k for k in range(seq_size)]

    def by_block(row):
        return jnp.concatenate([lax.dynamic_slice_in_dim(row, r * tokens, tokens) for r in rel])

    seg_all, valid_all = by_block(segment_ids[0]), by_block(valid_tokens[0])
    positions = by_block(jnp.arange(length, dtype=jnp.int32))
    frequency = ROPE_BASE ** (-2.0 * jnp.arange(HD // 2, dtype=F32) / HD)
    angles = positions.astype(F32)[:, None] * frequency[None, :]
    cosine, sine = lax.optimization_barrier((jnp.cos(angles), jnp.sin(angles)))
    cosine = jnp.concatenate([cosine] * 4, axis=1)
    sine = jnp.concatenate([-sine, sine] * 2, axis=1)
    seg_col, valid_col, seg_row = seg_all[:, None], valid_all[:, None], seg_all[None, :]

    first_mine = [lax.dynamic_slice_in_dim(w_qkv, i * D + seq * part, part, axis=1) for i in range(3)]
    first_mine.append(lax.dynamic_slice_in_dim(w_attn_out, seq * part, part, axis=1))
    gains = jnp.stack([attn_gain, mlp_gain], axis=1)
    first_mine.append(jnp.pad(gains, ((0, 0), (0, LANES - 2))))
    first_mine = jnp.concatenate(first_mine, axis=1)
    first_weight = gather_rows(first_mine)
    core = fsdp % 2
    slot = -(-hidden // LANES) * LANES
    if paired():
        down_mine = transpose_devices(lax.dynamic_slice_in_dim(w_out_proj, seq * part, part, axis=1))
    x_near = relay_first(x_low)
    out_mine = first_weight[:, 3 * part : 4 * part]
    gains = first_weight[:, 4 * part :].T.astype(F32)
    gain_one, gain_two = gains[0:1], gains[1:2]
    core = fsdp % 2
    slot = -(-hidden // LANES) * LANES
    def padded(rows):
        return jnp.pad(rows, ((0, 0), (0, slot - hidden)))

    def halves(rows):
        half = rows.shape[1] // 2
        low, high = rows[:, :half], rows[:, half:]
        return jnp.where(core == 0, low, high), jnp.where(core == 0, high, low)

    def by_core(mine, other):
        return jnp.where(core == 0, mine, other), jnp.where(core == 0, other, mine)

    in_mine = [
        padded(lax.dynamic_slice_in_dim(w_in_proj, i * FF + seq * hidden, hidden, axis=1)) for i in range(2)
    ]
    if paired():
        x_blocks = relay_last(x_low, *x_near)
        kept, sent = halves(after(down_mine, x_blocks, cosine, sine, seg_col, valid_col))
        down_mine = jnp.concatenate(by_core(kept, swap(sent, "fsdp", 1)), axis=0)
        feed_weight = gather_rows(jnp.concatenate(in_mine + [padded(down_mine.T)], axis=1))
    else:
        down_weight = lax.all_gather(w_out_proj, "fsdp", axis=0, tiled=True)
        down_weight = lax.dynamic_slice_in_dim(down_weight, seq * hidden, hidden, axis=0)
        feed_weight = jnp.concatenate([gather_rows(jnp.concatenate(in_mine, axis=1)), padded(down_weight.T)], axis=1)
        x_blocks = relay_last(x_low, *x_near)
    cot_near = relay_first(after(cot, *x_blocks))

    def in_order(blocks):
        bit = 1
        while bit < seq_size:
            flip = (seq & bit) != 0
            blocks = [jnp.where(flip, blocks[k ^ bit], blocks[k]) for k in range(seq_size)]
            bit *= 2
        return blocks


    a_low, q, k, v = project_qkv(x_blocks, first_weight, gain_one, cosine, sine)
    k, cot_near = after((k, cot_near), q)
    cot_blocks = relay_last(cot, *cot_near)
    mixed, lse = attend_forward(q, k, v, seg_col, valid_col, seg_row, tokens)

    out_near = relay_first(out_mine)
    mixed, out_near, cot_blocks = after((mixed, out_near, cot_blocks))
    out_weight = jnp.concatenate(in_order(relay_last(out_mine, *out_near)), axis=1)

    def to_tokens(blocks):
        came = [blocks[:tokens]] + [
            swap(blocks[i * tokens : (i + 1) * tokens], "seq", i) for i in range(1, seq_size)
        ]
        return jnp.concatenate(in_order(came), axis=1)

    mixed_low = to_tokens(mixed)
    x = x_low.astype(F32)
    attn_branch = matmul(mixed_low, out_weight)
    middle = x + attn_branch
    normed_two = (normal(middle)[0] * gain_two).astype(BF)
    normed_two = after(normed_two, *cot_blocks)

    b_blocks = share_seq(normed_two)
    fed, came, mlp_all = [None] * seq_size, [], None
    for i in range(seq_size):
        b = after(b_blocks[i], *came[:-1]) if len(came) > 1 else b_blocks[i]
        fed[i] = feed_forward(
            b, cot_blocks[i], feed_weight, hidden, seq, i, seq_size, F32 if i == 0 else BF, mlp_all
        )
        mlp_all = fed[i][4]
        if i > 0:
            came.append(swap(fed[i][3], "seq", i))
    m_blocks, gz_i, gz_g, gb_blocks, _ = zip(*fed)
    fed_grads = weight_gradients([after(b_blocks, *came[:-2])], [gz_i, gz_g], ((0, 1), (0, 2)), 3, 0)
    fed_grads = weight_gradients([after(cot_blocks, *came)], [m_blocks], ((0, 1),), 3, 2, fed_grads)
    grad_normed_two = gb_blocks[0]
    for block in came:
        grad_normed_two = grad_normed_two + block.astype(F32)
    grad_middle = cot.astype(F32) + norm_back(grad_normed_two, gain_two, middle)
    grad_attn_low = grad_middle.astype(BF)
    grad_mixed = matmul_nt(grad_attn_low, out_weight).astype(BF)

    sent = [lax.dynamic_slice_in_dim(grad_mixed, r * part, part, axis=1) for r in rel]
    came = [sent[0]] + [swap(sent[i], "seq", i) for i in range(1, seq_size)]
    grad_by_heads = jnp.concatenate(came, axis=0)
    out_part = matmul_tn(mixed_low, after(grad_attn_low, grad_by_heads)).astype(BF)
    grad_by_heads = after(grad_by_heads, out_part)
    mlp_came = exchange_seq(after(mlp_all, grad_by_heads))

    def own_rows(partial):
        return lax.psum_scatter(partial, "fsdp", scatter_dimension=0, tiled=True)

    fed_rows = own_rows(fed_grads)
    out_rows = own_rows(out_part)

    gp = attend_backward(
        q, k, v, grad_by_heads, lse, seg_col, valid_col, seg_row, cosine, sine, tokens
    )
    fed_late = after(fed_rows, gp)
    in_rows, down_rows = fed_late[:, : 2 * slot], fed_late[:, 2 * slot :]
    in_all = share_seq(in_rows)
    if paired():
        down_rows = transpose_devices(down_rows)
        ga_parts = project_back(gp, first_weight, seq, seq_size)
        gp_late = after(gp, ga_parts, *in_all[1:])
        ga_parts, down_rows = after((ga_parts, down_rows))
        mine, away = last_gradients(a_low, gp_late, fsdp, fsdp_size)
    else:
        mine, ga_parts = matmul_tn(a_low, gp), project_back(gp, first_weight, seq, seq_size)
        away = mine
    mlp_branch = sum_blocks(after(mlp_came, away))
    result = middle + mlp_branch
    valid_mine = valid_all[:tokens].astype(F32)[:, None]
    stats = jnp.stack(
        [
            jnp.sum(valid_mine * result * result),
            jnp.sum(valid_mine * attn_branch * attn_branch),
            jnp.sum(valid_mine * mlp_branch * mlp_branch),
            jnp.sum(valid_mine),
        ]
    )

    def sum_bit(values, bit):
        rows = jnp.broadcast_to(values[:, None], (values.shape[0], LANES))
        return values + swap(rows, "fsdp", bit)[:, 0]

    if paired():
        mine = mine + swap(away, "fsdp", 1).astype(F32)
        down_rows = after(down_rows, mine)
        kept, sent = halves(down_rows[:, :hidden])
        down_rows = jnp.concatenate(by_core(kept, swap(sent, "fsdp", 1)), axis=0).T
        rows = mine.shape[0] // (fsdp_size // 2)
        terms = in_three(sum_bit(stats, 1))
        extra = jnp.pad(terms, ((0, 16 - 3), (0, mine.shape[1] - 4)))
        came = [
            swap(jnp.concatenate([mine[k * rows : (k + 1) * rows].astype(BF), extra]), "fsdp", 2 * k)
            for k in range(1, fsdp_size // 2)
        ]
        ga_came = exchange_seq(ga_parts)
        came, ga_came = after((came, ga_came), down_rows, out_rows)
        last = mine[:rows]
        for block in came:
            last = last + block[:rows].astype(F32)
        stats = tree_sum([from_three(terms)] + [from_three(block[rows : rows + 3, :4]) for block in came])
    else:
        last = lax.psum_scatter(mine, "fsdp", scatter_dimension=0, tiled=True)
        ga_came = exchange_seq(ga_parts)
        bit = 1
        while bit < fsdp_size:
            stats = sum_bit(stats, bit)
            bit *= 2
    extra = jnp.pad(in_three(stats), ((0, last.shape[0] - 3), (0, LANES - 4)))
    last = jnp.concatenate([last.astype(BF), out_rows, extra], axis=1)
    ga_came, in_all, down_rows = after((ga_came, in_all, down_rows), last)

    grad_in_weight, grad_gain_two = finish_rows(
        functools.partial(in_rows_kernel, seq_size, hidden), in_all, w_in_proj, mlp_gain, seq, (2 * FF,), "in_rows"
    )
    if paired():
        grad_down = jnp.concatenate(in_order(share_seq(down_rows)), axis=1).astype(F32)
    else:
        down = lax.all_gather(down_rows[:, :hidden], ("seq", "fsdp"), axis=0, tiled=True)
        down = down.reshape(seq_size, D, hidden).transpose(0, 2, 1).reshape(FF, D)
        rows = FF // fsdp_size
        grad_down = lax.dynamic_slice_in_dim(down, fsdp * rows, rows, axis=0).astype(F32)

    grad_normed = sum_blocks(ga_came)
    grad_inputs = grad_middle + norm_back(grad_normed, gain_one, x)
    last = after(share_seq(last), grad_in_weight, grad_down, grad_inputs)
    grad_qkv_weight, grad_out_weight, grad_gain_one = finish_rows(
        functools.partial(last_rows_kernel, seq_size), last, w_qkv, attn_gain, seq, (3 * D, D), "last_rows"
    )

    stats = tree_sum([from_three(rows[:3, -LANES : 4 - LANES]) for rows in last])
    root_means = jnp.sqrt(stats[:3] / (jnp.maximum(stats[3], 1.0) * D))

    return (
        result.astype(BF)[None],
        grad_inputs[None],
        grad_qkv_weight,
        grad_out_weight,
        grad_in_weight,
        grad_down,
        grad_gain_one[0],
        grad_gain_two[0],
        root_means,
    )


def solution(mesh):
    in_specs = (
        P("fsdp", "seq", None),
        P("fsdp", None),
        P("fsdp", None),
        P("fsdp", None),
        P("fsdp", None),
        P("fsdp", None),
        P("fsdp", None),
        P("fsdp"),
        P("fsdp"),
        P("fsdp", "seq", None),
    )
    out_specs = (
        P("fsdp", "seq", None),
        P("fsdp", "seq", None),
        P("fsdp", None),
        P("fsdp", None),
        P("fsdp", None),
        P("fsdp", None),
        P("fsdp"),
        P("fsdp"),
        P(),
    )
    return jax.shard_map(on_device, mesh=mesh, in_specs=in_specs, out_specs=out_specs, check_vma=False)
```

profile of v0, /device:TPU:0, one launch (start us, length us, event | category | flops | bytes accessed | tf_op | source)
XLA Modules:
  0.0 355.0 jit_solution(17987576748521661223)
XLA Ops:
  12.3 3.1 collective-permute-start.1
  24.3 3.8 %collective-permute-done.1.refs_2_ = bf16[256,1024]{1,0:T(8,128)(2,1)S(1)} collective-permute-done((bf16[256,1024]{1,0:T(8,128)(2,1)}, bf16[256,1024]{1,0:T(8,128)(2,1)S(1)}, u32[]{:S(2)}, u32[]{:S(2)}) %collective-permute-start.1) | collective-permute-done | bytes 524320 | tf_op jit(solution)/shard_map/ppermute | solution.py:23
  28.1 4.6 %collective-permute-start.2 = (bf16[128,1024]{1,0:T(8,128)(2,1)S(1)}, bf16[128,1024]{1,0:T(8,128)(2,1)S(1)}, u32[]{:S(2)}, u32[]{:S(2)}) collective-permute-start(bf16[128,1024]{1,0:T(8,128)(2,1)S(1)} %slice.290), channel_id=1, source_target_pairs={{0,8},{8,0},{16,24},{24,16},{1,9},{9,1},{17,25},{25,17},{2,10},{10... | collective-permute-start | bytes 786440 | tf_op jit(solution)/shard_map/ppermute | solution.py:23
  32.7 4.3 %collective-permute-done.refs_1_ = bf16[256,1024]{1,0:T(8,128)(2,1)} collective-permute-done((bf16[256,1024]{1,0:T(8,128)(2,1)}, bf16[256,1024]{1,0:T(8,128)(2,1)}, u32[]{:S(2)}, u32[]{:S(2)}) %collective-permute-start) | collective-permute-done | bytes 524320 | tf_op jit(solution)/shard_map/ppermute | solution.py:23
  49.8 5.0 %all-gather.3.cloned.1.call-done.refs_4_.w_ref = bf16[1024,1152]{1,0:T(8,128)(2,1)} async-done(((bf16[128,1152]{1,0:T(8,128)(2,1)}), bf16[1024,1152]{1,0:T(8,128)(2,1)}) %all-gather.3.cloned.1.call-update) | async-done | bytes 2359312 | tf_op jit(solution)/shard_map/all_gather | solution.py:63
  59.0 7.2 %qkv.1 = (bf16[1024,1024]{1,0:T(8,128)(2,1)}, bf16[1024,256]{1,0:T(8,128)(2,1)}, bf16[1024,256]{1,0:T(8,128)(2,1)}, bf16[1024,256]{1,0:T(8,128)(2,1)}) custom-call(bf16[256,1024]{1,0:T(8,128)(2,1)} %bitcast.64, bf16[256,1024]{1,0:T(8,128)(2,1)} %collective-permute-done.refs_1_, bf16[256,1024]{1,0:T(8,128)(2,1)} %copy-done.24, bf16[256,1024]{1,0:T(8,128)(2,1)} %copy-done.25, ...), custom_call_target="tpu_custom_call" | custom-call | flops 1610612736 | bytes 7340032 | tf_op jit(solution)/shard_map/qkv/pallas_call | solution.py:140
  72.6 19.1 %attend.1 = (bf16[1024,256]{1,0:T(8,128)(2,1)}, f32[8,1024]{1,0:T(8,128)}) custom-call(bf16[1024,256]{1,0:T(8,128)(2,1)} %get-tuple-element.91.q_ref, bf16[1024,256]{1,0:T(8,128)(2,1)} %get-tuple-element.94.k_ref, bf16[1024,256]{1,0:T(8,128)(2,1)} %get-tuple-element.95.v_ref, s32[1024,1]{1,0:T(8,128)} %copy.39.segc_ref, s32[1024,1]{1,0:T(8,128)} %copy.40.valc_ref, ...), custom_call_target="tpu_custom_call" | custom-call | flops 1073741824 | bytes 2097152 | tf_op jit(solution)/shard_map/attend/pallas_call | solution.py:199
  98.8 5.3 %collective-permute-done.12 = bf16[256,256]{1,0:T(8,128)(2,1)S(1)} collective-permute-done((bf16[256,256]{1,0:T(8,128)(2,1)S(1)}, bf16[256,256]{1,0:T(8,128)(2,1)S(1)}, u32[]{:S(2)}, u32[]{:S(2)}) %collective-permute-start.12) | collective-permute-done | bytes 131104 | tf_op jit(solution)/shard_map/ppermute | solution.py:23
  117.6 6.7 %feed.4 = (bf16[256,656]{1,0:T(8,128)(2,1)}, bf16[256,656]{1,0:T(8,128)(2,1)}, bf16[256,656]{1,0:T(8,128)(2,1)}, f32[256,1024]{1,0:T(8,128)}, bf16[1024,1024]{1,0:T(8,128)(2,1)}) custom-call(s32[1]{0:T(128)} %bitcast.16.me_ref, bf16[256,1024]{1,0:T(8,128)(2,1)} %multiply_convert_fusion.b_ref.refs_0_, bf16[256,1024]{1,0:T(8,128)(2,1)} %bitcast.65, ...), custom_call_target="tpu_custom_call" | custom-call | flops 2063597568 | bytes 7135232 | tf_op jit(solution)/shard_map/feed/pallas_call | solution.py:331
  124.3 4.8 %collective-permute-done.16.b_ref.refs_1_ = bf16[256,1024]{1,0:T(8,128)(2,1)S(1)} collective-permute-done((bf16[256,1024]{1,0:T(8,128)(2,1)}, bf16[256,1024]{1,0:T(8,128)(2,1)S(1)}, u32[]{:S(2)}, u32[]{:S(2)}) %collective-permute-start.16) | collective-permute-done | bytes 524320 | tf_op jit(solution)/shard_map/ppermute | solution.py:23
  129.9 6.5 %feed.5 = (bf16[256,656]{1,0:T(8,128)(2,1)}, bf16[256,656]{1,0:T(8,128)(2,1)}, bf16[256,656]{1,0:T(8,128)(2,1)}, bf16[256,1024]{1,0:T(8,128)(2,1)}, bf16[1024,1024]{1,0:T(8,128)(2,1)}) custom-call(s32[1]{0:T(128)} %bitcast.16.me_ref, bf16[256,1024]{1,0:T(8,128)(2,1)} %copy-done.18, bf16[256,1024]{1,0:T(8,128)(2,1)} %copy-done.6, ...), custom_call_target="tpu_custom_call", output_to_operand_aliasing={{4}: (4, {})} | custom-call | flops 2063597568 | bytes 7135232 | tf_op jit(solution)/shard_map/feed/pallas_call | solution.py:331
  137.5 6.6 %feed.6 = (bf16[256,656]{1,0:T(8,128)(2,1)}, bf16[256,656]{1,0:T(8,128)(2,1)}, bf16[256,656]{1,0:T(8,128)(2,1)}, bf16[256,1024]{1,0:T(8,128)(2,1)}, bf16[1024,1024]{1,0:T(8,128)(2,1)}) custom-call(s32[1]{0:T(128)} %bitcast.16.me_ref, bf16[256,1024]{1,0:T(8,128)(2,1)} %copy-done.19, bf16[256,1024]{1,0:T(8,128)(2,1)} %copy-done.5, ...), custom_call_target="tpu_custom_call", output_to_operand_aliasing={{4}: (4, {})} | custom-call | flops 2063597568 | bytes 7135232 | tf_op jit(solution)/shard_map/feed/pallas_call | solution.py:331
  144.4 4.9 %collective-permute-done.19 = bf16[256,1024]{1,0:T(8,128)(2,1)S(1)} collective-permute-done((bf16[256,1024]{1,0:T(8,128)(2,1)}, bf16[256,1024]{1,0:T(8,128)(2,1)S(1)}, u32[]{:S(2)}, u32[]{:S(2)}) %collective-permute-start.19) | collective-permute-done | bytes 524320 | tf_op jit(solution)/shard_map/ppermute | solution.py:23
  149.3 7.0 %feed.7 = (bf16[256,656]{1,0:T(8,128)(2,1)}, bf16[256,656]{1,0:T(8,128)(2,1)}, bf16[256,656]{1,0:T(8,128)(2,1)}, bf16[256,1024]{1,0:T(8,128)(2,1)}, bf16[1024,1024]{1,0:T(8,128)(2,1)}) custom-call(s32[1]{0:T(128)} %bitcast.16.me_ref, bf16[256,1024]{1,0:T(8,128)(2,1)} %collective-permute-done.15.b_ref.refs_3_, ...), custom_call_target="tpu_custom_call", output_to_operand_aliasing={{4}: (4, {})} | custom-call | flops 2063597568 | bytes 7135232 | tf_op jit(solution)/shard_map/feed/pallas_call | solution.py:331
  156.2 7.6 %weight_gradients.2.refs_8_ = bf16[1024,2304]{1,0:T(8,128)(2,1)} custom-call(bf16[256,1024]{1,0:T(8,128)(2,1)} %multiply_convert_fusion.b_ref.refs_0_, bf16[256,1024]{1,0:T(8,128)(2,1)} %copy-done.18, bf16[256,1024]{1,0:T(8,128)(2,1)} %copy-done.19, bf16[256,1024]{1,0:T(8,128)(2,1)} %collective-permute-done.15.b_ref.refs_3_, ...), custom_call_target="tpu_custom_call" | custom-call | flops 2751463424 | bytes 4784128 | tf_op jit(solution)/shard_map/weight_gradients/pallas_call | solution.py:383
  163.8 5.1 %collective-permute-done.22 = bf16[256,1024]{1,0:T(8,128)(2,1)S(1)} collective-permute-done((bf16[256,1024]{1,0:T(8,128)(2,1)}, bf16[256,1024]{1,0:T(8,128)(2,1)S(1)}, u32[]{:S(2)}, u32[]{:S(2)}) %collective-permute-start.22) | collective-permute-done | bytes 524320 | tf_op jit(solution)/shard_map/ppermute | solution.py:23
  168.9 5.8 %weight_gradients.3 = bf16[1024,2304]{1,0:T(8,128)(2,1)} custom-call(bf16[256,1024]{1,0:T(8,128)(2,1)} %bitcast.66, bf16[256,1024]{1,0:T(8,128)(2,1)} %copy-done.6, bf16[256,1024]{1,0:T(8,128)(2,1)} %copy-done.5, bf16[256,1024]{1,0:T(8,128)(2,1)} %pad_maximum_fusion.3.g_ref.refs_3_, ...), custom_call_target="tpu_custom_call", output_to_operand_aliasing={{}: (8, {})} | custom-call | flops 1375731712 | bytes 3440640 | tf_op jit(solution)/shard_map/weight_gradients/pallas_call | solution.py:383
  189.9 3.6 %all-to-all-start = ((bf16[4,256,1024]{2,1,0:T(8,128)(2,1)}), bf16[4,256,1024]{2,1,0:T(8,128)(2,1)S(1)}, u32[]{:S(2)}, u32[]{:S(2)}) async-start(bf16[4,256,1024]{2,1,0:T(8,128)(2,1)} %bitcast.18), calls=%async_computation | async-start | bytes 4194304 | tf_op jit(solution)/shard_map/all_to_all | solution.py:47
  193.5 24.0 %attend_back.1.gp_ref = bf16[1024,768]{1,0:T(8,128)(2,1)} custom-call(bf16[1024,256]{1,0:T(8,128)(2,1)} %get-tuple-element.91.q_ref, bf16[1024,256]{1,0:T(8,128)(2,1)} %pad_maximum_fusion.5.go_ref, f32[8,1024]{1,0:T(8,128)} %get-tuple-element.121.lse_ref, bf16[1024,256]{1,0:T(8,128)(2,1)} %get-tuple-element.94.k_ref, ...), custom_call_target="tpu_custom_call" | custom-call | flops 2684354560 | bytes 5242880 | tf_op jit(solution)/shard_map/attend_back/pallas_call | solution.py:266
  217.5 12.4 %reduce-scatter.3.cloned.1.call-done = bf16[128,2304]{1,0:T(8,128)(2,1)} async-done(((bf16[1024,2304]{1,0:T(8,128)(2,1)}), bf16[128,2304]{1,0:T(8,128)(2,1)}) %reduce-scatter.3.cloned.1.call-update) | async-done | bytes 589840 | tf_op jit(solution)/shard_map/reduce_scatter | solution.py:670
  234.5 5.4 %project_back.1 = bf16[1024,1024]{1,0:T(8,128)(2,1)} custom-call(s32[1]{0:T(128)} %bitcast.16.me_ref, bf16[1024,768]{1,0:T(8,128)(2,1)} %attend_back.1.gp_ref, bf16[1024,1152]{1,0:T(8,128)(2,1)} %all-gather.3.cloned.1.call-done.refs_4_.w_ref), custom_call_target="tpu_custom_call" | custom-call | flops 1610612736 | bytes 5242880 | tf_op jit(solution)/shard_map/project_back/pallas_call | solution.py:442
  241.5 3.0 collective-permute-start.34
  244.5 5.4 %collective-permute-done.27.refs_2_ = bf16[128,1536]{1,0:T(8,128)(2,1)} collective-permute-done((bf16[128,1536]{1,0:T(8,128)(2,1)S(1)}, bf16[128,1536]{1,0:T(8,128)(2,1)}, u32[]{:S(2)}, u32[]{:S(2)}) %collective-permute-start.27) | collective-permute-done | bytes 393248 | tf_op jit(solution)/shard_map/ppermute | solution.py:23
  251.8 8.2 %last_gradients.1 = (f32[512,768]{1,0:T(8,128)}, bf16[512,768]{1,0:T(8,128)(2,1)}) custom-call(s32[1]{0:T(128)} %bitcast.20.me_ref, bf16[1024,1024]{1,0:T(8,128)(2,1)} %get-tuple-element.120.a_ref, bf16[1024,768]{1,0:T(8,128)(2,1)} %attend_back.1.gp_ref), custom_call_target="tpu_custom_call" | custom-call | flops 1610612736 | bytes 6029312 | tf_op jit(solution)/shard_map/last_gradients/pallas_call | solution.py:415
  260.0 3.3 fusion.13
  266.5 4.1 %all-to-all-start.1 = ((bf16[4,256,1024]{2,1,0:T(8,128)(2,1)}), bf16[4,256,1024]{2,1,0:T(8,128)(2,1)S(1)}, u32[]{:S(2)}, u32[]{:S(2)}) async-start(bf16[4,256,1024]{2,1,0:T(8,128)(2,1)} %bitcast.31), calls=%async_computation.2 | async-start | bytes 4194304 | tf_op jit(solution)/shard_map/all_to_all | solution.py:47
  279.7 6.0 %collective-permute-start.32 = (bf16[144,768]{1,0:T(8,128)(2,1)S(1)}, bf16[144,768]{1,0:T(8,128)(2,1)}, u32[]{:S(2)}, u32[]{:S(2)}) collective-permute-start(bf16[144,768]{1,0:T(8,128)(2,1)S(1)} %get-tuple-element.262), channel_id=1, source_target_pairs={{0,4},{1,5},{2,6},{3,7},{4,0},{5,1},{6,2},{7,3},{8,12},{9,13},{10,... | collective-permute-start | bytes 663560 | tf_op jit(solution)/shard_map/ppermute | solution.py:23
  288.7 13.6 %collective-permute-done.32 = bf16[144,768]{1,0:T(8,128)(2,1)} collective-permute-done((bf16[144,768]{1,0:T(8,128)(2,1)S(1)}, bf16[144,768]{1,0:T(8,128)(2,1)}, u32[]{:S(2)}, u32[]{:S(2)}) %collective-permute-start.32) | collective-permute-done | bytes 221216 | tf_op jit(solution)/shard_map/ppermute | solution.py:23
  318.5 4.1 %in_rows.1 = (f32[128,5248]{1,0:T(8,128)}, f32[1,128]{1,0:T(1,128)}) custom-call(s32[1]{0:T(128)} %bitcast.16.me_ref, bf16[128,1536]{1,0:T(8,128)(2,1)} %copy-done.10, bf16[128,1536]{1,0:T(8,128)(2,1)} %collective-permute-done.26.refs_1_, bf16[128,1536]{1,0:T(8,128)(2,1)} %collective-permute-done.27.refs_2_, ...), custom_call_target="tpu_custom_call" | custom-call | bytes 5373952 | tf_op jit(solution)/shard_map/in_rows/pallas_call | solution.py:508
  322.6 9.4 %collective-permute-done.40 = bf16[328,256]{0,1:T(8,128)(2,1)} collective-permute-done((bf16[328,256]{0,1:T(8,128)(2,1)S(1)}, bf16[328,256]{0,1:T(8,128)(2,1)}, u32[]{:S(2)}, u32[]{:S(2)}) %collective-permute-start.40) | collective-permute-done | bytes 167968 | tf_op jit(solution)/shard_map/ppermute | solution.py:23
  334.8 6.5 %collective-permute-done.37.refs_2_ = bf16[128,1920]{1,0:T(8,128)(2,1)} collective-permute-done((bf16[128,1920]{1,0:T(8,128)(2,1)S(1)}, bf16[128,1920]{1,0:T(8,128)(2,1)}, u32[]{:S(2)}, u32[]{:S(2)}) %collective-permute-start.37) | collective-permute-done | bytes 491552 | tf_op jit(solution)/shard_map/ppermute | solution.py:23
  345.2 3.3 last_rows.1
  (250 shorter events, 120.5 us)
Async XLA Ops:
  7.2 47.6 %all-gather.3.cloned.1.call-start = ((), (), s32[]{:S(2)}) async-start(), calls=%async_computation.4 | async-start | bytes 2654208 | tf_op jit(solution)/shard_map/all_gather | solution.py:63
  12.3 105.4 %all-gather.5.cloned.1.call-start = ((), (), s32[]{:S(2)}) async-start(), calls=%async_computation.5 | async-start | bytes 5308416 | tf_op jit(solution)/shard_map/all_gather | solution.py:63
  12.3 15.7 %collective-permute-start.1 = (bf16[256,1024]{1,0:T(8,128)(2,1)}, bf16[256,1024]{1,0:T(8,128)(2,1)S(1)}, u32[]{:S(2)}, u32[]{:S(2)}) collective-permute-start(bf16[256,1024]{1,0:T(8,128)(2,1)} %bitcast.62), channel_id=1, source_target_pairs={{0,16},{8,24},{16,0},{24,8},{1,17},{9,25},{17,1},{25,9},{2,18},{10... | collective-permute-start | bytes 1572872 | tf_op jit(solution)/shard_map/ppermute | solution.py:23
  15.4 21.6 %collective-permute-start = (bf16[256,1024]{1,0:T(8,128)(2,1)}, bf16[256,1024]{1,0:T(8,128)(2,1)}, u32[]{:S(2)}, u32[]{:S(2)}) collective-permute-start(bf16[256,1024]{1,0:T(8,128)(2,1)} %bitcast.63), channel_id=1, source_target_pairs={{0,8},{8,0},{16,24},{24,16},{1,9},{9,1},{17,25},{25,17},{2,10},{10... | collective-permute-start | bytes 1572872 | tf_op jit(solution)/shard_map/ppermute | solution.py:23
  17.7 26.7 %collective-permute-start.17 = (bf16[328,256]{0,1:T(8,128)(2,1)}, bf16[328,256]{0,1:T(8,128)(2,1)S(1)}, u32[]{:S(2)}, u32[]{:S(2)}) collective-permute-start(bf16[328,256]{0,1:T(8,128)(2,1)} %copy.45), channel_id=1, source_target_pairs={{0,0},{1,1},{2,8},{3,9},{4,16},{5,17},{6,24},{7,25},{8,2},{9,3},{1... | collective-permute-start | bytes 503816 | tf_op jit(solution)/shard_map/ppermute | solution.py:74
  28.1 14.0 %collective-permute-start.2 = (bf16[128,1024]{1,0:T(8,128)(2,1)S(1)}, bf16[128,1024]{1,0:T(8,128)(2,1)S(1)}, u32[]{:S(2)}, u32[]{:S(2)}) collective-permute-start(bf16[128,1024]{1,0:T(8,128)(2,1)S(1)} %slice.290), channel_id=1, source_target_pairs={{0,8},{8,0},{16,24},{24,16},{1,9},{9,1},{17,25},{25,17},{2,10},{10... | collective-permute-start | bytes 786440 | tf_op jit(solution)/shard_map/ppermute | solution.py:23
  46.9 183.0 %reduce-scatter.3.cloned.1.call-start = ((), (), s32[]{:S(2)}) async-start(), calls=%async_computation.6 | async-start | bytes 5308416 | tf_op jit(solution)/shard_map/reduce_scatter | solution.py:670
  46.9 19.2 %collective-permute-start.5 = (bf16[256,1024]{1,0:T(8,128)(2,1)S(1)}, bf16[256,1024]{1,0:T(8,128)(2,1)S(1)}, u32[]{:S(2)}, u32[]{:S(2)}) collective-permute-start(bf16[256,1024]{1,0:T(8,128)(2,1)S(1)} %bitcast.67), channel_id=1, source_target_pairs={{0,16},{8,24},{16,0},{24,8},{1,17},{9,25},{17,1},{25,9},{2,18},{10... | collective-permute-start | bytes 1572872 | tf_op jit(solution)/shard_map/ppermute | solution.py:23
  47.5 18.7 %collective-permute-start.4 = (bf16[256,1024]{1,0:T(8,128)(2,1)S(1)}, bf16[256,1024]{1,0:T(8,128)(2,1)S(1)}, u32[]{:S(2)}, u32[]{:S(2)}) collective-permute-start(bf16[256,1024]{1,0:T(8,128)(2,1)S(1)} %bitcast.68), channel_id=1, source_target_pairs={{0,8},{8,0},{16,24},{24,16},{1,9},{9,1},{17,25},{25,17},{2,10},{10... | collective-permute-start | bytes 1572872 | tf_op jit(solution)/shard_map/ppermute | solution.py:23
  56.7 35.9 %collective-permute-start.7 = (bf16[1024,256]{1,0:T(8,128)(2,1)}, bf16[1024,256]{1,0:T(8,128)(2,1)S(1)}, u32[]{:S(2)}, u32[]{:S(2)}) collective-permute-start(bf16[1024,256]{1,0:T(8,128)(2,1)} %slice.294), channel_id=1, source_target_pairs={{0,16},{8,24},{16,0},{24,8},{1,17},{9,25},{17,1},{25,9},{2,18},{10... | collective-permute-start | bytes 1572872 | tf_op jit(solution)/shard_map/ppermute | solution.py:23
  56.7 35.9 %collective-permute-start.6 = (bf16[1024,256]{1,0:T(8,128)(2,1)}, bf16[1024,256]{1,0:T(8,128)(2,1)}, u32[]{:S(2)}, u32[]{:S(2)}) collective-permute-start(bf16[1024,256]{1,0:T(8,128)(2,1)} %slice.294), channel_id=1, source_target_pairs={{0,8},{8,0},{16,24},{24,16},{1,9},{9,1},{17,25},{25,17},{2,10},{10... | collective-permute-start | bytes 1572872 | tf_op jit(solution)/shard_map/ppermute | solution.py:23
  66.2 25.4 %collective-permute-start.8 = (bf16[128,1024]{1,0:T(8,128)(2,1)S(1)}, bf16[128,1024]{1,0:T(8,128)(2,1)S(1)}, u32[]{:S(2)}, u32[]{:S(2)}) collective-permute-start(bf16[128,1024]{1,0:T(8,128)(2,1)S(1)} %slice.224), channel_id=1, source_target_pairs={{0,8},{8,0},{16,24},{24,16},{1,9},{9,1},{17,25},{25,17},{2,10},{10... | collective-permute-start | bytes 786440 | tf_op jit(solution)/shard_map/ppermute | solution.py:23
  68.3 23.3 %collective-permute-start.9 = (bf16[128,1024]{1,0:T(8,128)(2,1)S(1)}, bf16[128,1024]{1,0:T(8,128)(2,1)S(1)}, u32[]{:S(2)}, u32[]{:S(2)}) collective-permute-start(bf16[128,1024]{1,0:T(8,128)(2,1)S(1)} %slice.225), channel_id=1, source_target_pairs={{0,16},{8,24},{16,0},{24,8},{1,17},{9,25},{17,1},{25,9},{2,18},{10... | collective-permute-start | bytes 786440 | tf_op jit(solution)/shard_map/ppermute | solution.py:23
  92.5 13.7 %collective-permute-start.13 = (bf16[512,256]{1,0:T(8,128)(2,1)S(1)}, bf16[512,256]{1,0:T(8,128)(2,1)S(1)}, u32[]{:S(2)}, u32[]{:S(2)}) collective-permute-start(bf16[512,256]{1,0:T(8,128)(2,1)S(1)} %slice.230), channel_id=1, source_target_pairs={{0,8},{8,0},{16,24},{24,16},{1,9},{9,1},{17,25},{25,17},{2,10},{10... | collective-permute-start | bytes 786440 | tf_op jit(solution)/shard_map/ppermute | solution.py:23
  114.1 15.0 %collective-permute-start.16 = (bf16[256,1024]{1,0:T(8,128)(2,1)}, bf16[256,1024]{1,0:T(8,128)(2,1)S(1)}, u32[]{:S(2)}, u32[]{:S(2)}) collective-permute-start(bf16[256,1024]{1,0:T(8,128)(2,1)} %multiply_convert_fusion.b_ref.refs_0_), channel_id=1, source_target_pairs={{0,8},{8,0},{16,24},{24,16},{1,9},{9,1},{17,25},{25,17},{2,10},{10... | collective-permute-start | bytes 1572872 | tf_op jit(solution)/shard_map/ppermute | solution.py:23
  114.4 22.4 %collective-permute-start.20 = (bf16[256,1024]{1,0:T(8,128)(2,1)}, bf16[256,1024]{1,0:T(8,128)(2,1)S(1)}, u32[]{:S(2)}, u32[]{:S(2)}) collective-permute-start(bf16[256,1024]{1,0:T(8,128)(2,1)} %multiply_convert_fusion.b_ref.refs_0_), channel_id=1, source_target_pairs={{0,16},{8,24},{16,0},{24,8},{1,17},{9,25},{17,1},{25,9},{2,18},{10... | collective-permute-start | bytes 1572872 | tf_op jit(solution)/shard_map/ppermute | solution.py:23
  114.7 29.7 %collective-permute-start.15 = (bf16[256,1024]{1,0:T(8,128)(2,1)}, bf16[256,1024]{1,0:T(8,128)(2,1)}, u32[]{:S(2)}, u32[]{:S(2)}) collective-permute-start(bf16[256,1024]{1,0:T(8,128)(2,1)} %multiply_convert_fusion.b_ref.refs_0_), channel_id=1, source_target_pairs={{0,24},{8,16},{16,8},{24,0},{1,25},{9,17},{17,9},{25,1},{2,26},{10... | collective-permute-start | bytes 1572872 | tf_op jit(solution)/shard_map/ppermute | solution.py:23
  144.1 19.7 %collective-permute-start.21 = (bf16[256,1024]{1,0:T(8,128)(2,1)}, bf16[256,1024]{1,0:T(8,128)(2,1)S(1)}, u32[]{:S(2)}, u32[]{:S(2)}) collective-permute-start(bf16[256,1024]{1,0:T(8,128)(2,1)} %get-tuple-element.115), channel_id=1, source_target_pairs={{0,16},{8,24},{16,0},{24,8},{1,17},{9,25},{17,1},{25,9},{2,18},{10... | collective-permute-start | bytes 1572872 | tf_op jit(solution)/shard_map/ppermute | solution.py:23
  174.7 112.0 %reduce-scatter.5.cloned.1.call-start = ((), (), s32[]{:S(2)}) async-start(), calls=%async_computation.7 | async-start | bytes 2359296 | tf_op jit(solution)/shard_map/reduce_scatter | solution.py:670
  189.9 70.1 %all-to-all-start = ((bf16[4,256,1024]{2,1,0:T(8,128)(2,1)}), bf16[4,256,1024]{2,1,0:T(8,128)(2,1)S(1)}, u32[]{:S(2)}, u32[]{:S(2)}) async-start(bf16[4,256,1024]{2,1,0:T(8,128)(2,1)} %bitcast.18), calls=%async_computation | async-start | bytes 4194304 | tf_op jit(solution)/shard_map/all_to_all | solution.py:47
  230.9 13.6 %collective-permute-start.28 = (bf16[128,1536]{1,0:T(8,128)(2,1)S(1)}, bf16[128,1536]{1,0:T(8,128)(2,1)}, u32[]{:S(2)}, u32[]{:S(2)}) collective-permute-start(bf16[128,1536]{1,0:T(8,128)(2,1)S(1)} %slice.235.refs_0_), channel_id=1, source_target_pairs={{0,24},{8,16},{16,8},{24,0},{1,25},{9,17},{17,9},{25,1},{2,26},{10... | collective-permute-start | bytes 1179656 | tf_op jit(solution)/shard_map/ppermute | solution.py:23
  233.4 16.5 %collective-permute-start.27 = (bf16[128,1536]{1,0:T(8,128)(2,1)S(1)}, bf16[128,1536]{1,0:T(8,128)(2,1)}, u32[]{:S(2)}, u32[]{:S(2)}) collective-permute-start(bf16[128,1536]{1,0:T(8,128)(2,1)S(1)} %slice.235.refs_0_), channel_id=1, source_target_pairs={{0,16},{8,24},{16,0},{24,8},{1,17},{9,25},{17,1},{25,9},{2,18},{10... | collective-permute-start | bytes 1179656 | tf_op jit(solution)/shard_map/ppermute | solution.py:23
  233.9 17.9 %collective-permute-start.26 = (bf16[128,1536]{1,0:T(8,128)(2,1)S(1)}, bf16[128,1536]{1,0:T(8,128)(2,1)}, u32[]{:S(2)}, u32[]{:S(2)}) collective-permute-start(bf16[128,1536]{1,0:T(8,128)(2,1)S(1)} %slice.235.refs_0_), channel_id=1, source_target_pairs={{0,8},{8,0},{16,24},{24,16},{1,9},{9,1},{17,25},{25,17},{2,10},{10... | collective-permute-start | bytes 1179656 | tf_op jit(solution)/shard_map/ppermute | solution.py:23
  241.5 25.0 %collective-permute-start.34 = (bf16[128,768]{1,0:T(8,128)(2,1)}, bf16[128,768]{1,0:T(8,128)(2,1)}, u32[]{:S(2)}, u32[]{:S(2)}) collective-permute-start(bf16[128,768]{1,0:T(8,128)(2,1)} %slice.244), channel_id=1, source_target_pairs={{0,0},{1,1},{2,8},{3,9},{4,16},{5,17},{6,24},{7,25},{8,2},{9,3},{1... | collective-permute-start | bytes 589832 | tf_op jit(solution)/shard_map/ppermute | solution.py:74
  266.5 35.8 %all-to-all-start.1 = ((bf16[4,256,1024]{2,1,0:T(8,128)(2,1)}), bf16[4,256,1024]{2,1,0:T(8,128)(2,1)S(1)}, u32[]{:S(2)}, u32[]{:S(2)}) async-start(bf16[4,256,1024]{2,1,0:T(8,128)(2,1)} %bitcast.31), calls=%async_computation.2 | async-start | bytes 4194304 | tf_op jit(solution)/shard_map/all_to_all | solution.py:47
  279.7 22.7 %collective-permute-start.32 = (bf16[144,768]{1,0:T(8,128)(2,1)S(1)}, bf16[144,768]{1,0:T(8,128)(2,1)}, u32[]{:S(2)}, u32[]{:S(2)}) collective-permute-start(bf16[144,768]{1,0:T(8,128)(2,1)S(1)} %get-tuple-element.262), channel_id=1, source_target_pairs={{0,4},{1,5},{2,6},{3,7},{4,0},{5,1},{6,2},{7,3},{8,12},{9,13},{10,... | collective-permute-start | bytes 663560 | tf_op jit(solution)/shard_map/ppermute | solution.py:23
  285.6 16.8 %collective-permute-start.31 = (bf16[144,768]{1,0:T(8,128)(2,1)S(1)}, bf16[144,768]{1,0:T(8,128)(2,1)}, u32[]{:S(2)}, u32[]{:S(2)}) collective-permute-start(bf16[144,768]{1,0:T(8,128)(2,1)S(1)} %get-tuple-element.263), channel_id=1, source_target_pairs={{0,2},{1,3},{2,0},{3,1},{4,6},{5,7},{6,4},{7,5},{8,10},{9,11},{10,... | collective-permute-start | bytes 663560 | tf_op jit(solution)/shard_map/ppermute | solution.py:23
  309.4 22.6 %collective-permute-start.40 = (bf16[328,256]{0,1:T(8,128)(2,1)S(1)}, bf16[328,256]{0,1:T(8,128)(2,1)}, u32[]{:S(2)}, u32[]{:S(2)}) collective-permute-start(bf16[328,256]{0,1:T(8,128)(2,1)S(1)} %maximum_bitcast_fusion.1), channel_id=1, source_target_pairs={{0,16},{8,24},{16,0},{24,8},{1,17},{9,25},{17,1},{25,9},{2,18},{10... | collective-permute-start | bytes 503816 | tf_op jit(solution)/shard_map/ppermute | solution.py:23
  310.3 21.7 %collective-permute-start.39 = (bf16[328,256]{0,1:T(8,128)(2,1)S(1)}, bf16[328,256]{0,1:T(8,128)(2,1)}, u32[]{:S(2)}, u32[]{:S(2)}) collective-permute-start(bf16[328,256]{0,1:T(8,128)(2,1)S(1)} %maximum_bitcast_fusion.1), channel_id=1, source_target_pairs={{0,24},{8,16},{16,8},{24,0},{1,25},{9,17},{17,9},{25,1},{2,26},{10... | collective-permute-start | bytes 503816 | tf_op jit(solution)/shard_map/ppermute | solution.py:23
  311.0 23.9 %collective-permute-start.38 = (bf16[128,1920]{1,0:T(8,128)(2,1)S(1)}, bf16[128,1920]{1,0:T(8,128)(2,1)}, u32[]{:S(2)}, u32[]{:S(2)}) collective-permute-start(bf16[128,1920]{1,0:T(8,128)(2,1)S(1)} %pad_maximum_fusion.6.refs_0_), channel_id=1, source_target_pairs={{0,24},{8,16},{16,8},{24,0},{1,25},{9,17},{17,9},{25,1},{2,26},{10... | collective-permute-start | bytes 1474568 | tf_op jit(solution)/shard_map/ppermute | solution.py:23
  313.3 28.1 %collective-permute-start.37 = (bf16[128,1920]{1,0:T(8,128)(2,1)S(1)}, bf16[128,1920]{1,0:T(8,128)(2,1)}, u32[]{:S(2)}, u32[]{:S(2)}) collective-permute-start(bf16[128,1920]{1,0:T(8,128)(2,1)S(1)} %pad_maximum_fusion.6.refs_0_), channel_id=1, source_target_pairs={{0,16},{8,24},{16,0},{24,8},{1,17},{9,25},{17,1},{25,9},{2,18},{10... | collective-permute-start | bytes 1474568 | tf_op jit(solution)/shard_map/ppermute | solution.py:23
  315.2 26.2 %collective-permute-start.36 = (bf16[128,1920]{1,0:T(8,128)(2,1)S(1)}, bf16[128,1920]{1,0:T(8,128)(2,1)}, u32[]{:S(2)}, u32[]{:S(2)}) collective-permute-start(bf16[128,1920]{1,0:T(8,128)(2,1)S(1)} %pad_maximum_fusion.6.refs_0_), channel_id=1, source_target_pairs={{0,8},{8,0},{16,24},{24,16},{1,9},{9,1},{17,25},{25,17},{2,10},{10... | collective-permute-start | bytes 1474568 | tf_op jit(solution)/shard_map/ppermute | solution.py:23
  (48 other events, 529.6 us)
Sparse Core Ops, SparseCore 0:
  12.4 42.3 all-gather.2
  57.0 51.5 all-gather.4
  174.8 54.9 reduce-scatter.2
  232.0 42.6 reduce-scatter.4
where the time goes:
time: 357 us; the launch traced here: 355 us
  Pallas kernels  111 us (31%)
  waiting for transfers between devices  96.2 us (27%)
  starting transfers between devices  61.7 us (17%)
  other arithmetic  41.2 us (12%)
  local copies, waits for them, and re-layouts  24.3 us (7%)
  between operations  15.1 us (4%)
  matrix products  5.1 us (1%)
    ppermute x40, waiting for transfers between devices, swap(): lax.ppermute(x, axis, [(i, i ^ bit) for i in range(lax.axis_size(axis))])  78.8 us
    ppermute x40, starting transfers between devices, swap(): lax.ppermute(x, axis, [(i, i ^ bit) for i in range(lax.axis_size(axis))])  49.3 us
    pallas_call x4, Pallas kernels, feed_forward(): pl.pallas_call(functools.partial(feed_kernel, hidden), grid_spec=pltpu.Pr...  26.8 us
    pallas_call x1, Pallas kernels, attend_backward(): pl.pallas_call(backward_kernel, grid=(length // rows,), in_specs=[tile, t...  24 us
    pallas_call x1, Pallas kernels, attend_forward(): pl.pallas_call(forward_kernel, grid=(length // rows,), in_specs=[tile, wh...  19.1 us
    pallas_call x2, Pallas kernels, weight_gradients(): pl.pallas_call(functools.partial(weight_kernel, count, slot, pairs), grid...  13.3 us
    reduce_scatter x2, waiting for transfers between devices, own_rows(): return lax.psum_scatter(partial, 'fsdp', scatter_dimension=0, tiled=True)  12.4 us
    unnamed x72, local copies, waits for them, and re-layouts  9.32 us
  transfers between devices with their start and end apart: 48, of which 22 were waited for; matrix products, arithmetic and copies ran while one was open for 16% of the time, Pallas kernels for 29%

commit v1 on v0

--- a/solution.py
+++ b/solution.py
@@ -675,18 +675,10 @@
     gp = attend_backward(
         q, k, v, grad_by_heads, lse, seg_col, valid_col, seg_row, cosine, sine, tokens
     )
-    fed_late = after(fed_rows, gp)
-    in_rows, down_rows = fed_late[:, : 2 * slot], fed_late[:, 2 * slot :]
-    in_all = share_seq(in_rows)
     if paired():
-        down_rows = transpose_devices(down_rows)
-        ga_parts = project_back(gp, first_weight, seq, seq_size)
-        gp_late = after(gp, ga_parts, *in_all[1:])
-        ga_parts, down_rows = after((ga_parts, down_rows))
-        mine, away = last_gradients(a_low, gp_late, fsdp, fsdp_size)
+        mine, away = last_gradients(a_low, gp, fsdp, fsdp_size)
     else:
-        mine, ga_parts = matmul_tn(a_low, gp), project_back(gp, first_weight, seq, seq_size)
-        away = mine
+        mine = away = matmul_tn(a_low, gp)
     mlp_branch = sum_blocks(after(mlp_came, away))
     result = middle + mlp_branch
     valid_mine = valid_all[:tokens].astype(F32)[:, None]
@@ -703,28 +695,31 @@
         rows = jnp.broadcast_to(values[:, None], (values.shape[0], LANES))
         return values + swap(rows, "fsdp", bit)[:, 0]
 
+    stats = sum_bit(stats, 1)
+    gp_late, stats = after((gp, stats))
+    fed_late, stats = after((fed_rows, stats))
+    in_rows, down_rows = fed_late[:, : 2 * slot], fed_late[:, 2 * slot :]
+    in_all = share_seq(in_rows)
+    ga_parts = project_back(gp_late, first_weight, seq, seq_size)
+    ga_came = exchange_seq(after(ga_parts, *in_all[1:3]))
     if paired():
-        mine = mine + swap(away, "fsdp", 1).astype(F32)
-        down_rows = after(down_rows, mine)
-        kept, sent = halves(down_rows[:, :hidden])
-        down_rows = jnp.concatenate(by_core(kept, swap(sent, "fsdp", 1)), axis=0).T
+        mine = mine + after(swap(away, "fsdp", 1), ga_parts).astype(F32)
+        down_rows = transpose_devices(down_rows)
         rows = mine.shape[0] // (fsdp_size // 2)
-        terms = in_three(sum_bit(stats, 1))
+        terms = in_three(stats)
         extra = jnp.pad(terms, ((0, 16 - 3), (0, mine.shape[1] - 4)))
         came = [
             swap(jnp.concatenate([mine[k * rows : (k + 1) * rows].astype(BF), extra]), "fsdp", 2 * k)
             for k in range(1, fsdp_size // 2)
         ]
-        ga_came = exchange_seq(ga_parts)
-        came, ga_came = after((came, ga_came), down_rows, out_rows)
+        came, ga_came = after((came, ga_came), out_rows)
         last = mine[:rows]
         for block in came:
             last = last + block[:rows].astype(F32)
         stats = tree_sum([from_three(terms)] + [from_three(block[rows : rows + 3, :4]) for block in came])
     else:
         last = lax.psum_scatter(mine, "fsdp", scatter_dimension=0, tiled=True)
-        ga_came = exchange_seq(ga_parts)
-        bit = 1
+        bit = 2
         while bit < fsdp_size:
             stats = sum_bit(stats, bit)
             bit *= 2
@@ -736,6 +731,8 @@
         functools.partial(in_rows_kernel, seq_size, hidden), in_all, w_in_proj, mlp_gain, seq, (2 * FF,), "in_rows"
     )
     if paired():
+        kept, sent = halves(down_rows[:, :hidden])
+        down_rows = jnp.concatenate(by_core(kept, swap(sent, "fsdp", 1)), axis=0).T
         grad_down = jnp.concatenate(in_order(share_seq(down_rows)), axis=1).astype(F32)
     else:
         down = lax.all_gather(down_rows[:, :hidden], ("seq", "fsdp"), axis=0, tiled=True)

time: 357 us -> 346 us (0.969)
  waiting for transfers between devices: 96.2 us -> 88.2 us
    reduce_scatter x2, waiting for transfers between devices: 12.4 us -> 0.01 us  [own_rows(): return lax.psum_scatter(partial, 'fsdp', scatter_dimension=0, tiled=True)]
    ppermute x40, waiting for transfers between devices: 78.8 us -> 83.4 us  [swap(): lax.ppermute(x, axis, [(i, i ^ bit) for i in range(lax.axis_size(axis))])]
    unnamed x72 -> x74, local copies, waits for them, and re-layouts: 9.32 us -> 7.96 us
  transfers between devices with their start and end apart: 48 -> 48, of which waited for: 22 -> 23; matrix products, arithmetic and copies ran while one was open for 16% -> 16% of each run, Pallas kernels for 29% -> 30%
where the time goes in v1:
time: 346 us; the launch traced here: 342 us
  Pallas kernels  111 us (32%)
  waiting for transfers between devices  88.2 us (25%)
  starting transfers between devices  60.9 us (18%)
  other arithmetic  39.4 us (11%)
  local copies, waits for them, and re-layouts  22.7 us (7%)
  between operations  15.2 us (4%)
  matrix products  4.34 us (1%)
    ppermute x40, waiting for transfers between devices, swap(): lax.ppermute(x, axis, [(i, i ^ bit) for i in range(lax.axis_size(axis))])  83.4 us
    ppermute x40, starting transfers between devices, swap(): lax.ppermute(x, axis, [(i, i ^ bit) for i in range(lax.axis_size(axis))])  50.4 us
    pallas_call x4, Pallas kernels, feed_forward(): pl.pallas_call(functools.partial(feed_kernel, hidden), grid_spec=pltpu.Pr...  26.6 us
    pallas_call x1, Pallas kernels, attend_backward(): pl.pallas_call(backward_kernel, grid=(length // rows,), in_specs=[tile, t...  24 us
    pallas_call x1, Pallas kernels, attend_forward(): pl.pallas_call(forward_kernel, grid=(length // rows,), in_specs=[tile, wh...  19.1 us
    pallas_call x2, Pallas kernels, weight_gradients(): pl.pallas_call(functools.partial(weight_kernel, count, slot, pairs), grid...  13.1 us
    pallas_call x1, Pallas kernels, last_gradients(): pl.pallas_call(last_kernel, grid_spec=pltpu.PrefetchScalarGridSpec(num_sc...  8.15 us
    all_to_all x2, starting transfers between devices, exchange_seq(): lax.all_to_all(blocks, 'seq', split_axis=0, concat_axis=0, tiled=True)  8.08 us
  transfers between devices with their start and end apart: 48, of which 23 were waited for; matrix products, arithmetic and copies ran while one was open for 16% of the time, Pallas kernels for 30%

profile of v1, /device:TPU:0, one launch (start us, length us, event | category | flops | bytes accessed | tf_op | source)
XLA Modules:
  0.0 341.8 jit_solution(6882680973794515253)
XLA Ops:
  12.3 3.1 collective-permute-start.1
  22.7 5.7 %collective-permute-done.1.refs_2_ = bf16[256,1024]{1,0:T(8,128)(2,1)S(1)} collective-permute-done((bf16[256,1024]{1,0:T(8,128)(2,1)}, bf16[256,1024]{1,0:T(8,128)(2,1)S(1)}, u32[]{:S(2)}, u32[]{:S(2)}) %collective-permute-start.1) | collective-permute-done | bytes 524320 | tf_op jit(solution)/shard_map/ppermute | solution.py:23
  28.5 4.2 %collective-permute-start.2 = (bf16[128,1024]{1,0:T(8,128)(2,1)S(1)}, bf16[128,1024]{1,0:T(8,128)(2,1)S(1)}, u32[]{:S(2)}, u32[]{:S(2)}) collective-permute-start(bf16[128,1024]{1,0:T(8,128)(2,1)S(1)} %slice.290), channel_id=1, source_target_pairs={{0,8},{8,0},{16,24},{24,16},{1,9},{9,1},{17,25},{25,17},{2,10},{10... | collective-permute-start | bytes 786440 | tf_op jit(solution)/shard_map/ppermute | solution.py:23
  32.7 4.4 %collective-permute-done.refs_1_ = bf16[256,1024]{1,0:T(8,128)(2,1)} collective-permute-done((bf16[256,1024]{1,0:T(8,128)(2,1)}, bf16[256,1024]{1,0:T(8,128)(2,1)}, u32[]{:S(2)}, u32[]{:S(2)}) %collective-permute-start) | collective-permute-done | bytes 524320 | tf_op jit(solution)/shard_map/ppermute | solution.py:23
  49.9 4.0 %all-gather.3.cloned.1.call-done.refs_4_.w_ref = bf16[1024,1152]{1,0:T(8,128)(2,1)} async-done(((bf16[128,1152]{1,0:T(8,128)(2,1)}), bf16[1024,1152]{1,0:T(8,128)(2,1)}) %all-gather.3.cloned.1.call-update) | async-done | bytes 2359312 | tf_op jit(solution)/shard_map/all_gather | solution.py:63
  58.1 7.2 %qkv.1 = (bf16[1024,1024]{1,0:T(8,128)(2,1)}, bf16[1024,256]{1,0:T(8,128)(2,1)}, bf16[1024,256]{1,0:T(8,128)(2,1)}, bf16[1024,256]{1,0:T(8,128)(2,1)}) custom-call(bf16[256,1024]{1,0:T(8,128)(2,1)} %bitcast.73, bf16[256,1024]{1,0:T(8,128)(2,1)} %collective-permute-done.refs_1_, bf16[256,1024]{1,0:T(8,128)(2,1)} %copy-done.25, bf16[256,1024]{1,0:T(8,128)(2,1)} %copy-done.26, ...), custom_call_target="tpu_custom_call" | custom-call | flops 1610612736 | bytes 7340032 | tf_op jit(solution)/shard_map/qkv/pallas_call | solution.py:140
  71.7 19.1 %attend.1 = (bf16[1024,256]{1,0:T(8,128)(2,1)}, f32[8,1024]{1,0:T(8,128)}) custom-call(bf16[1024,256]{1,0:T(8,128)(2,1)} %get-tuple-element.92.q_ref, bf16[1024,256]{1,0:T(8,128)(2,1)} %get-tuple-element.95.k_ref, bf16[1024,256]{1,0:T(8,128)(2,1)} %get-tuple-element.96.v_ref, s32[1024,1]{1,0:T(8,128)} %copy.39.segc_ref, s32[1024,1]{1,0:T(8,128)} %copy.40.valc_ref, ...), custom_call_target="tpu_custom_call" | custom-call | flops 1073741824 | bytes 2097152 | tf_op jit(solution)/shard_map/attend/pallas_call | solution.py:199
  98.0 6.3 %collective-permute-done.12 = bf16[256,256]{1,0:T(8,128)(2,1)S(1)} collective-permute-done((bf16[256,256]{1,0:T(8,128)(2,1)S(1)}, bf16[256,256]{1,0:T(8,128)(2,1)S(1)}, u32[]{:S(2)}, u32[]{:S(2)}) %collective-permute-start.12) | collective-permute-done | bytes 131104 | tf_op jit(solution)/shard_map/ppermute | solution.py:23
  115.9 6.7 %feed.4 = (bf16[256,656]{1,0:T(8,128)(2,1)}, bf16[256,656]{1,0:T(8,128)(2,1)}, bf16[256,656]{1,0:T(8,128)(2,1)}, f32[256,1024]{1,0:T(8,128)}, bf16[1024,1024]{1,0:T(8,128)(2,1)}) custom-call(s32[1]{0:T(128)} %bitcast.16.me_ref, bf16[256,1024]{1,0:T(8,128)(2,1)} %multiply_convert_fusion.b_ref.refs_0_, bf16[256,1024]{1,0:T(8,128)(2,1)} %bitcast.74, ...), custom_call_target="tpu_custom_call" | custom-call | flops 2063597568 | bytes 7135232 | tf_op jit(solution)/shard_map/feed/pallas_call | solution.py:331
  122.6 4.8 %collective-permute-done.16.b_ref.refs_1_ = bf16[256,1024]{1,0:T(8,128)(2,1)S(1)} collective-permute-done((bf16[256,1024]{1,0:T(8,128)(2,1)}, bf16[256,1024]{1,0:T(8,128)(2,1)S(1)}, u32[]{:S(2)}, u32[]{:S(2)}) %collective-permute-start.16) | collective-permute-done | bytes 524320 | tf_op jit(solution)/shard_map/ppermute | solution.py:23
  128.2 6.6 %feed.5 = (bf16[256,656]{1,0:T(8,128)(2,1)}, bf16[256,656]{1,0:T(8,128)(2,1)}, bf16[256,656]{1,0:T(8,128)(2,1)}, bf16[256,1024]{1,0:T(8,128)(2,1)}, bf16[1024,1024]{1,0:T(8,128)(2,1)}) custom-call(s32[1]{0:T(128)} %bitcast.16.me_ref, bf16[256,1024]{1,0:T(8,128)(2,1)} %copy-done.17, bf16[256,1024]{1,0:T(8,128)(2,1)} %copy-done.5, ...), custom_call_target="tpu_custom_call", output_to_operand_aliasing={{4}: (4, {})} | custom-call | flops 2063597568 | bytes 7135232 | tf_op jit(solution)/shard_map/feed/pallas_call | solution.py:331
  135.9 6.5 %feed.6 = (bf16[256,656]{1,0:T(8,128)(2,1)}, bf16[256,656]{1,0:T(8,128)(2,1)}, bf16[256,656]{1,0:T(8,128)(2,1)}, bf16[256,1024]{1,0:T(8,128)(2,1)}, bf16[1024,1024]{1,0:T(8,128)(2,1)}) custom-call(s32[1]{0:T(128)} %bitcast.16.me_ref, bf16[256,1024]{1,0:T(8,128)(2,1)} %collective-permute-done.20.b_ref.refs_2_, ...), custom_call_target="tpu_custom_call", output_to_operand_aliasing={{4}: (4, {})} | custom-call | flops 2063597568 | bytes 7135232 | tf_op jit(solution)/shard_map/feed/pallas_call | solution.py:331
  142.4 4.6 %collective-permute-done.19 = bf16[256,1024]{1,0:T(8,128)(2,1)S(1)} collective-permute-done((bf16[256,1024]{1,0:T(8,128)(2,1)}, bf16[256,1024]{1,0:T(8,128)(2,1)S(1)}, u32[]{:S(2)}, u32[]{:S(2)}) %collective-permute-start.19) | collective-permute-done | bytes 524320 | tf_op jit(solution)/shard_map/ppermute | solution.py:23
  147.0 6.8 %feed.7 = (bf16[256,656]{1,0:T(8,128)(2,1)}, bf16[256,656]{1,0:T(8,128)(2,1)}, bf16[256,656]{1,0:T(8,128)(2,1)}, bf16[256,1024]{1,0:T(8,128)(2,1)}, bf16[1024,1024]{1,0:T(8,128)(2,1)}) custom-call(s32[1]{0:T(128)} %bitcast.16.me_ref, bf16[256,1024]{1,0:T(8,128)(2,1)} %collective-permute-done.15.b_ref.refs_3_, ...), custom_call_target="tpu_custom_call", output_to_operand_aliasing={{4}: (4, {})} | custom-call | flops 2063597568 | bytes 7135232 | tf_op jit(solution)/shard_map/feed/pallas_call | solution.py:331
  154.5 7.6 %weight_gradients.2.refs_8_ = bf16[1024,2304]{1,0:T(8,128)(2,1)} custom-call(bf16[256,1024]{1,0:T(8,128)(2,1)} %multiply_convert_fusion.b_ref.refs_0_, bf16[256,1024]{1,0:T(8,128)(2,1)} %copy-done.17, bf16[256,1024]{1,0:T(8,128)(2,1)} %collective-permute-done.20.b_ref.refs_2_, bf16[256,1024]{1,0:T(8,128)(2,1)} %collective-permute-done.15.b_ref.refs_3_, ...), custom_call_target="tpu_custom_call" | custom-call | flops 2751463424 | bytes 4784128 | tf_op jit(solution)/shard_map/weight_gradients/pallas_call | solution.py:383
  162.1 4.0 %collective-permute-done.22 = bf16[256,1024]{1,0:T(8,128)(2,1)} collective-permute-done((bf16[256,1024]{1,0:T(8,128)(2,1)}, bf16[256,1024]{1,0:T(8,128)(2,1)}, u32[]{:S(2)}, u32[]{:S(2)}) %collective-permute-start.22) | collective-permute-done | bytes 524320 | tf_op jit(solution)/shard_map/ppermute | solution.py:23
  166.0 5.6 %weight_gradients.3 = bf16[1024,2304]{1,0:T(8,128)(2,1)} custom-call(bf16[256,1024]{1,0:T(8,128)(2,1)} %bitcast.75, bf16[256,1024]{1,0:T(8,128)(2,1)} %copy-done.5, bf16[256,1024]{1,0:T(8,128)(2,1)} %copy-done.4, bf16[256,1024]{1,0:T(8,128)(2,1)} %pad_maximum_fusion.3.g_ref.refs_3_, ...), custom_call_target="tpu_custom_call", output_to_operand_aliasing={{}: (8, {})} | custom-call | flops 1375731712 | bytes 3440640 | tf_op jit(solution)/shard_map/weight_gradients/pallas_call | solution.py:383
  177.5 2.9 collective-permute-start.24
  188.4 4.5 %all-to-all-start = ((bf16[4,256,1024]{2,1,0:T(8,128)(2,1)}), bf16[4,256,1024]{2,1,0:T(8,128)(2,1)}, u32[]{:S(2)}, u32[]{:S(2)}) async-start(bf16[4,256,1024]{2,1,0:T(8,128)(2,1)} %bitcast.18), calls=%async_computation | async-start | bytes 4194304 | tf_op jit(solution)/shard_map/all_to_all | solution.py:47
  192.9 24.0 %attend_back.1.gp_ref = bf16[1024,768]{1,0:T(8,128)(2,1)} custom-call(bf16[1024,256]{1,0:T(8,128)(2,1)} %get-tuple-element.92.q_ref, bf16[1024,256]{1,0:T(8,128)(2,1)} %pad_maximum_fusion.5.go_ref, f32[8,1024]{1,0:T(8,128)} %get-tuple-element.122.lse_ref, bf16[1024,256]{1,0:T(8,128)(2,1)} %get-tuple-element.95.k_ref, ...), custom_call_target="tpu_custom_call" | custom-call | flops 2684354560 | bytes 5242880 | tf_op jit(solution)/shard_map/attend_back/pallas_call | solution.py:266
  216.9 8.2 %last_gradients.1 = (f32[512,768]{1,0:T(8,128)}, bf16[512,768]{1,0:T(8,128)(2,1)}) custom-call(s32[1]{0:T(128)} %bitcast.20.me_ref, bf16[1024,1024]{1,0:T(8,128)(2,1)} %get-tuple-element.121.a_ref, bf16[1024,768]{1,0:T(8,128)(2,1)} %attend_back.1.gp_ref), custom_call_target="tpu_custom_call" | custom-call | flops 1610612736 | bytes 6029312 | tf_op jit(solution)/shard_map/last_gradients/pallas_call | solution.py:415
  225.0 3.6 %fusion.13 = (f32[]{:T(128)}, f32[]{:T(128)}, f32[]{:T(128)}, bf16[1,256,1024]{2,1,0:T(8,128)(2,1)}) fusion(f32[256]{0:T(256)S(1)} %convert_element_type.155, f32[256,1024]{1,0:T(8,128)S(1)} %get-tuple-element.220, bf16[1024,1024]{1,0:T(8,128)(2,1)} %bitcast.19, f32[256,1024]{1,0:T(8,128)S(1)} %get-tuple-element.269), kind=kLoop, calls=%fused_computation.27 | loop fusion | flops 4718589 | bytes 4719628 | tf_op jit(solution)/shard_map/reduce_sum | solution.py:687
  240.5 5.4 %project_back.1 = bf16[1024,1024]{1,0:T(8,128)(2,1)} custom-call(s32[1]{0:T(128)} %bitcast.16.me_ref, bf16[1024,768]{1,0:T(8,128)(2,1)} %attend_back.1.gp_ref, bf16[1024,1152]{1,0:T(8,128)(2,1)} %all-gather.3.cloned.1.call-done.refs_4_.w_ref), custom_call_target="tpu_custom_call" | custom-call | flops 1610612736 | bytes 5242880 | tf_op jit(solution)/shard_map/project_back/pallas_call | solution.py:442
  245.9 2.8 collective-permute-done.32.refs_2_
  250.9 3.6 %all-to-all-start.1 = ((bf16[4,256,1024]{2,1,0:T(8,128)(2,1)}), bf16[4,256,1024]{2,1,0:T(8,128)(2,1)S(1)}, u32[]{:S(2)}, u32[]{:S(2)}) async-start(bf16[4,256,1024]{2,1,0:T(8,128)(2,1)} %bitcast.69), calls=%async_computation.2 | async-start | bytes 4194304 | tf_op jit(solution)/shard_map/all_to_all | solution.py:47
  258.1 3.3 collective-permute-start.30
  264.1 2.9 collective-permute-start.33
  268.7 17.4 %collective-permute-done.29 = bf16[144,768]{1,0:T(8,128)(2,1)} collective-permute-done((bf16[144,768]{1,0:T(8,128)(2,1)S(1)}, bf16[144,768]{1,0:T(8,128)(2,1)}, u32[]{:S(2)}, u32[]{:S(2)}) %collective-permute-start.29) | collective-permute-done | bytes 221216 | tf_op jit(solution)/shard_map/ppermute | solution.py:23
  291.2 3.3 collective-permute-start.37
  301.0 17.9 %collective-permute-done.41 = bf16[328,256]{0,1:T(8,128)(2,1)S(1)} collective-permute-done((bf16[328,256]{0,1:T(8,128)(2,1)S(1)}, bf16[328,256]{0,1:T(8,128)(2,1)S(1)}, u32[]{:S(2)}, u32[]{:S(2)}) %collective-permute-start.41) | collective-permute-done | bytes 167968 | tf_op jit(solution)/shard_map/ppermute | solution.py:23
  322.1 4.1 %in_rows.1 = (f32[128,5248]{1,0:T(8,128)}, f32[1,128]{1,0:T(1,128)}) custom-call(s32[1]{0:T(128)} %bitcast.16.me_ref, bf16[128,1536]{1,0:T(8,128)(2,1)} %slice.243.refs_0_, bf16[128,1536]{1,0:T(8,128)(2,1)} %copy-done.20, bf16[128,1536]{1,0:T(8,128)(2,1)} %copy-done.19, bf16[128,1536]{1,0:T(8,128)(2,1)} %collective-permute-done.33.refs_3_, ...), custom_call_target="tpu_custom_call" | custom-call | bytes 5373952 | tf_op jit(solution)/shard_map/in_rows/pallas_call | solution.py:508
  331.9 3.3 last_rows.1
  (252 shorter events, 112.3 us)
Async XLA Ops:
  7.2 46.8 %all-gather.3.cloned.1.call-start = ((), (), s32[]{:S(2)}) async-start(), calls=%async_computation.4 | async-start | bytes 2654208 | tf_op jit(solution)/shard_map/all_gather | solution.py:63
  12.3 103.6 %all-gather.5.cloned.1.call-start = ((), (), s32[]{:S(2)}) async-start(), calls=%async_computation.5 | async-start | bytes 5308416 | tf_op jit(solution)/shard_map/all_gather | solution.py:63
  12.3 16.2 %collective-permute-start.1 = (bf16[256,1024]{1,0:T(8,128)(2,1)}, bf16[256,1024]{1,0:T(8,128)(2,1)S(1)}, u32[]{:S(2)}, u32[]{:S(2)}) collective-permute-start(bf16[256,1024]{1,0:T(8,128)(2,1)} %bitcast.71), channel_id=1, source_target_pairs={{0,16},{8,24},{16,0},{24,8},{1,17},{9,25},{17,1},{25,9},{2,18},{10... | collective-permute-start | bytes 1572872 | tf_op jit(solution)/shard_map/ppermute | solution.py:23
  15.4 21.8 %collective-permute-start = (bf16[256,1024]{1,0:T(8,128)(2,1)}, bf16[256,1024]{1,0:T(8,128)(2,1)}, u32[]{:S(2)}, u32[]{:S(2)}) collective-permute-start(bf16[256,1024]{1,0:T(8,128)(2,1)} %bitcast.72), channel_id=1, source_target_pairs={{0,8},{8,0},{16,24},{24,16},{1,9},{9,1},{17,25},{25,17},{2,10},{10... | collective-permute-start | bytes 1572872 | tf_op jit(solution)/shard_map/ppermute | solution.py:23
  17.1 27.5 %collective-permute-start.17 = (bf16[328,256]{0,1:T(8,128)(2,1)S(1)}, bf16[328,256]{0,1:T(8,128)(2,1)S(1)}, u32[]{:S(2)}, u32[]{:S(2)}) collective-permute-start(bf16[328,256]{0,1:T(8,128)(2,1)S(1)} %copy.45), channel_id=1, source_target_pairs={{0,0},{1,1},{2,8},{3,9},{4,16},{5,17},{6,24},{7,25},{8,2},{9,3},{1... | collective-permute-start | bytes 503816 | tf_op jit(solution)/shard_map/ppermute | solution.py:74
  28.5 13.5 %collective-permute-start.2 = (bf16[128,1024]{1,0:T(8,128)(2,1)S(1)}, bf16[128,1024]{1,0:T(8,128)(2,1)S(1)}, u32[]{:S(2)}, u32[]{:S(2)}) collective-permute-start(bf16[128,1024]{1,0:T(8,128)(2,1)S(1)} %slice.290), channel_id=1, source_target_pairs={{0,8},{8,0},{16,24},{24,16},{1,9},{9,1},{17,25},{25,17},{2,10},{10... | collective-permute-start | bytes 786440 | tf_op jit(solution)/shard_map/ppermute | solution.py:23
  47.0 188.2 %reduce-scatter.3.cloned.1.call-start = ((), (), s32[]{:S(2)}) async-start(), calls=%async_computation.6 | async-start | bytes 5308416 | tf_op jit(solution)/shard_map/reduce_scatter | solution.py:670
  47.1 18.2 %collective-permute-start.5 = (bf16[256,1024]{1,0:T(8,128)(2,1)S(1)}, bf16[256,1024]{1,0:T(8,128)(2,1)S(1)}, u32[]{:S(2)}, u32[]{:S(2)}) collective-permute-start(bf16[256,1024]{1,0:T(8,128)(2,1)S(1)} %bitcast.76), channel_id=1, source_target_pairs={{0,16},{8,24},{16,0},{24,8},{1,17},{9,25},{17,1},{25,9},{2,18},{10... | collective-permute-start | bytes 1572872 | tf_op jit(solution)/shard_map/ppermute | solution.py:23
  47.4 17.9 %collective-permute-start.4 = (bf16[256,1024]{1,0:T(8,128)(2,1)S(1)}, bf16[256,1024]{1,0:T(8,128)(2,1)S(1)}, u32[]{:S(2)}, u32[]{:S(2)}) collective-permute-start(bf16[256,1024]{1,0:T(8,128)(2,1)S(1)} %bitcast.77), channel_id=1, source_target_pairs={{0,8},{8,0},{16,24},{24,16},{1,9},{9,1},{17,25},{25,17},{2,10},{10... | collective-permute-start | bytes 1572872 | tf_op jit(solution)/shard_map/ppermute | solution.py:23
  55.8 36.8 %collective-permute-start.7 = (bf16[1024,256]{1,0:T(8,128)(2,1)}, bf16[1024,256]{1,0:T(8,128)(2,1)S(1)}, u32[]{:S(2)}, u32[]{:S(2)}) collective-permute-start(bf16[1024,256]{1,0:T(8,128)(2,1)} %slice.294), channel_id=1, source_target_pairs={{0,16},{8,24},{16,0},{24,8},{1,17},{9,25},{17,1},{25,9},{2,18},{10... | collective-permute-start | bytes 1572872 | tf_op jit(solution)/shard_map/ppermute | solution.py:23
  55.8 36.8 %collective-permute-start.6 = (bf16[1024,256]{1,0:T(8,128)(2,1)}, bf16[1024,256]{1,0:T(8,128)(2,1)S(1)}, u32[]{:S(2)}, u32[]{:S(2)}) collective-permute-start(bf16[1024,256]{1,0:T(8,128)(2,1)} %slice.294), channel_id=1, source_target_pairs={{0,8},{8,0},{16,24},{24,16},{1,9},{9,1},{17,25},{25,17},{2,10},{10... | collective-permute-start | bytes 1572872 | tf_op jit(solution)/shard_map/ppermute | solution.py:23
  65.4 25.4 %collective-permute-start.8 = (bf16[128,1024]{1,0:T(8,128)(2,1)S(1)}, bf16[128,1024]{1,0:T(8,128)(2,1)S(1)}, u32[]{:S(2)}, u32[]{:S(2)}) collective-permute-start(bf16[128,1024]{1,0:T(8,128)(2,1)S(1)} %slice.224), channel_id=1, source_target_pairs={{0,8},{8,0},{16,24},{24,16},{1,9},{9,1},{17,25},{25,17},{2,10},{10... | collective-permute-start | bytes 786440 | tf_op jit(solution)/shard_map/ppermute | solution.py:23
  67.5 23.3 %collective-permute-start.9 = (bf16[128,1024]{1,0:T(8,128)(2,1)S(1)}, bf16[128,1024]{1,0:T(8,128)(2,1)}, u32[]{:S(2)}, u32[]{:S(2)}) collective-permute-start(bf16[128,1024]{1,0:T(8,128)(2,1)S(1)} %slice.225), channel_id=1, source_target_pairs={{0,16},{8,24},{16,0},{24,8},{1,17},{9,25},{17,1},{25,9},{2,18},{10... | collective-permute-start | bytes 786440 | tf_op jit(solution)/shard_map/ppermute | solution.py:23
  92.6 13.8 %collective-permute-start.13 = (bf16[512,256]{1,0:T(8,128)(2,1)S(1)}, bf16[512,256]{1,0:T(8,128)(2,1)S(1)}, u32[]{:S(2)}, u32[]{:S(2)}) collective-permute-start(bf16[512,256]{1,0:T(8,128)(2,1)S(1)} %slice.230), channel_id=1, source_target_pairs={{0,8},{8,0},{16,24},{24,16},{1,9},{9,1},{17,25},{25,17},{2,10},{10... | collective-permute-start | bytes 786440 | tf_op jit(solution)/shard_map/ppermute | solution.py:23
  112.4 15.0 %collective-permute-start.16 = (bf16[256,1024]{1,0:T(8,128)(2,1)}, bf16[256,1024]{1,0:T(8,128)(2,1)S(1)}, u32[]{:S(2)}, u32[]{:S(2)}) collective-permute-start(bf16[256,1024]{1,0:T(8,128)(2,1)} %multiply_convert_fusion.b_ref.refs_0_), channel_id=1, source_target_pairs={{0,8},{8,0},{16,24},{24,16},{1,9},{9,1},{17,25},{25,17},{2,10},{10... | collective-permute-start | bytes 1572872 | tf_op jit(solution)/shard_map/ppermute | solution.py:23
  113.5 22.4 %collective-permute-start.20 = (bf16[256,1024]{1,0:T(8,128)(2,1)}, bf16[256,1024]{1,0:T(8,128)(2,1)}, u32[]{:S(2)}, u32[]{:S(2)}) collective-permute-start(bf16[256,1024]{1,0:T(8,128)(2,1)} %multiply_convert_fusion.b_ref.refs_0_), channel_id=1, source_target_pairs={{0,16},{8,24},{16,0},{24,8},{1,17},{9,25},{17,1},{25,9},{2,18},{10... | collective-permute-start | bytes 1572872 | tf_op jit(solution)/shard_map/ppermute | solution.py:23
  113.5 28.9 %collective-permute-start.15 = (bf16[256,1024]{1,0:T(8,128)(2,1)}, bf16[256,1024]{1,0:T(8,128)(2,1)}, u32[]{:S(2)}, u32[]{:S(2)}) collective-permute-start(bf16[256,1024]{1,0:T(8,128)(2,1)} %multiply_convert_fusion.b_ref.refs_0_), channel_id=1, source_target_pairs={{0,24},{8,16},{16,8},{24,0},{1,25},{9,17},{17,9},{25,1},{2,26},{10... | collective-permute-start | bytes 1572872 | tf_op jit(solution)/shard_map/ppermute | solution.py:23
  134.7 12.2 %collective-permute-start.19 = (bf16[256,1024]{1,0:T(8,128)(2,1)}, bf16[256,1024]{1,0:T(8,128)(2,1)S(1)}, u32[]{:S(2)}, u32[]{:S(2)}) collective-permute-start(bf16[256,1024]{1,0:T(8,128)(2,1)} %get-tuple-element.110), channel_id=1, source_target_pairs={{0,8},{8,0},{16,24},{24,16},{1,9},{9,1},{17,25},{25,17},{2,10},{10... | collective-permute-start | bytes 1572872 | tf_op jit(solution)/shard_map/ppermute | solution.py:23
  142.4 19.7 %collective-permute-start.21 = (bf16[256,1024]{1,0:T(8,128)(2,1)}, bf16[256,1024]{1,0:T(8,128)(2,1)}, u32[]{:S(2)}, u32[]{:S(2)}) collective-permute-start(bf16[256,1024]{1,0:T(8,128)(2,1)} %get-tuple-element.116), channel_id=1, source_target_pairs={{0,16},{8,24},{16,0},{24,8},{1,17},{9,25},{17,1},{25,9},{2,18},{10... | collective-permute-start | bytes 1572872 | tf_op jit(solution)/shard_map/ppermute | solution.py:23
  171.6 96.9 %reduce-scatter.5.cloned.1.call-start = ((), (), s32[]{:S(2)}) async-start(), calls=%async_computation.7 | async-start | bytes 2359296 | tf_op jit(solution)/shard_map/reduce_scatter | solution.py:670
  188.4 36.6 %all-to-all-start = ((bf16[4,256,1024]{2,1,0:T(8,128)(2,1)}), bf16[4,256,1024]{2,1,0:T(8,128)(2,1)}, u32[]{:S(2)}, u32[]{:S(2)}) async-start(bf16[4,256,1024]{2,1,0:T(8,128)(2,1)} %bitcast.18), calls=%async_computation | async-start | bytes 4194304 | tf_op jit(solution)/shard_map/all_to_all | solution.py:47
  231.3 23.2 %collective-permute-start.26 = (bf16[512,768]{1,0:T(8,128)(2,1)}, bf16[512,768]{1,0:T(8,128)(2,1)S(1)}, u32[]{:S(2)}, u32[]{:S(2)}) collective-permute-start(bf16[512,768]{1,0:T(8,128)(2,1)} %get-tuple-element.123), channel_id=1, source_target_pairs={{0,1},{1,0},{2,3},{3,2},{4,5},{5,4},{6,7},{7,6},{8,9},{9,8},{10,11... | collective-permute-start | bytes 2359304 | tf_op jit(solution)/shard_map/ppermute | solution.py:23
  250.9 35.9 %all-to-all-start.1 = ((bf16[4,256,1024]{2,1,0:T(8,128)(2,1)}), bf16[4,256,1024]{2,1,0:T(8,128)(2,1)S(1)}, u32[]{:S(2)}, u32[]{:S(2)}) async-start(bf16[4,256,1024]{2,1,0:T(8,128)(2,1)} %bitcast.69), calls=%async_computation.2 | async-start | bytes 4194304 | tf_op jit(solution)/shard_map/all_to_all | solution.py:47
  261.4 24.7 %collective-permute-start.29 = (bf16[144,768]{1,0:T(8,128)(2,1)S(1)}, bf16[144,768]{1,0:T(8,128)(2,1)}, u32[]{:S(2)}, u32[]{:S(2)}) collective-permute-start(bf16[144,768]{1,0:T(8,128)(2,1)S(1)} %get-tuple-element.262), channel_id=1, source_target_pairs={{0,4},{1,5},{2,6},{3,7},{4,0},{5,1},{6,2},{7,3},{8,12},{9,13},{10,... | collective-permute-start | bytes 663560 | tf_op jit(solution)/shard_map/ppermute | solution.py:23
  261.8 24.3 %collective-permute-start.28 = (bf16[144,768]{1,0:T(8,128)(2,1)S(1)}, bf16[144,768]{1,0:T(8,128)(2,1)}, u32[]{:S(2)}, u32[]{:S(2)}) collective-permute-start(bf16[144,768]{1,0:T(8,128)(2,1)S(1)} %get-tuple-element.263), channel_id=1, source_target_pairs={{0,2},{1,3},{2,0},{3,1},{4,6},{5,7},{6,4},{7,5},{8,10},{9,11},{10,... | collective-permute-start | bytes 663560 | tf_op jit(solution)/shard_map/ppermute | solution.py:23
  264.1 31.2 %collective-permute-start.33 = (bf16[128,1536]{1,0:T(8,128)(2,1)}, bf16[128,1536]{1,0:T(8,128)(2,1)}, u32[]{:S(2)}, u32[]{:S(2)}) collective-permute-start(bf16[128,1536]{1,0:T(8,128)(2,1)} %slice.243.refs_0_), channel_id=1, source_target_pairs={{0,24},{8,16},{16,8},{24,0},{1,25},{9,17},{17,9},{25,1},{2,26},{10... | collective-permute-start | bytes 1179656 | tf_op jit(solution)/shard_map/ppermute | solution.py:23
  267.0 28.2 %collective-permute-start.34 = (bf16[128,768]{1,0:T(8,128)(2,1)}, bf16[128,768]{1,0:T(8,128)(2,1)S(1)}, u32[]{:S(2)}, u32[]{:S(2)}) collective-permute-start(bf16[128,768]{1,0:T(8,128)(2,1)} %slice.244), channel_id=1, source_target_pairs={{0,0},{1,1},{2,8},{3,9},{4,16},{5,17},{6,24},{7,25},{8,2},{9,3},{1... | collective-permute-start | bytes 589832 | tf_op jit(solution)/shard_map/ppermute | solution.py:74
  291.2 36.9 %collective-permute-start.37 = (bf16[128,1920]{1,0:T(8,128)(2,1)S(1)}, bf16[128,1920]{1,0:T(8,128)(2,1)}, u32[]{:S(2)}, u32[]{:S(2)}) collective-permute-start(bf16[128,1920]{1,0:T(8,128)(2,1)S(1)} %pad_maximum_fusion.6.refs_0_), channel_id=1, source_target_pairs={{0,24},{8,16},{16,8},{24,0},{1,25},{9,17},{17,9},{25,1},{2,26},{10... | collective-permute-start | bytes 1474568 | tf_op jit(solution)/shard_map/ppermute | solution.py:23
  294.5 33.6 %collective-permute-start.36 = (bf16[128,1920]{1,0:T(8,128)(2,1)S(1)}, bf16[128,1920]{1,0:T(8,128)(2,1)}, u32[]{:S(2)}, u32[]{:S(2)}) collective-permute-start(bf16[128,1920]{1,0:T(8,128)(2,1)S(1)} %pad_maximum_fusion.6.refs_0_), channel_id=1, source_target_pairs={{0,16},{8,24},{16,0},{24,8},{1,17},{9,25},{17,1},{25,9},{2,18},{10... | collective-permute-start | bytes 1474568 | tf_op jit(solution)/shard_map/ppermute | solution.py:23
  294.5 33.6 %collective-permute-start.35 = (bf16[128,1920]{1,0:T(8,128)(2,1)S(1)}, bf16[128,1920]{1,0:T(8,128)(2,1)}, u32[]{:S(2)}, u32[]{:S(2)}) collective-permute-start(bf16[128,1920]{1,0:T(8,128)(2,1)S(1)} %pad_maximum_fusion.6.refs_0_), channel_id=1, source_target_pairs={{0,8},{8,0},{16,24},{24,16},{1,9},{9,1},{17,25},{25,17},{2,10},{10... | collective-permute-start | bytes 1474568 | tf_op jit(solution)/shard_map/ppermute | solution.py:23
  296.9 22.0 %collective-permute-start.41 = (bf16[328,256]{0,1:T(8,128)(2,1)S(1)}, bf16[328,256]{0,1:T(8,128)(2,1)S(1)}, u32[]{:S(2)}, u32[]{:S(2)}) collective-permute-start(bf16[328,256]{0,1:T(8,128)(2,1)S(1)} %maximum_bitcast_fusion.1), channel_id=1, source_target_pairs={{0,8},{8,0},{16,24},{24,16},{1,9},{9,1},{17,25},{25,17},{2,10},{10... | collective-permute-start | bytes 503816 | tf_op jit(solution)/shard_map/ppermute | solution.py:23
  298.2 28.0 %collective-permute-start.40 = (bf16[328,256]{0,1:T(8,128)(2,1)S(1)}, bf16[328,256]{0,1:T(8,128)(2,1)S(1)}, u32[]{:S(2)}, u32[]{:S(2)}) collective-permute-start(bf16[328,256]{0,1:T(8,128)(2,1)S(1)} %maximum_bitcast_fusion.1), channel_id=1, source_target_pairs={{0,16},{8,24},{16,0},{24,8},{1,17},{9,25},{17,1},{25,9},{2,18},{10... | collective-permute-start | bytes 503816 | tf_op jit(solution)/shard_map/ppermute | solution.py:23
  (49 other events, 429.1 us)
Sparse Core Ops, SparseCore 0:
  12.4 41.5 all-gather.2
  56.2 51.4 all-gather.4
  171.7 56.1 reduce-scatter.2
  230.1 35.4 reduce-scatter.4

commit v2 on v1

--- a/solution.py
+++ b/solution.py
@@ -730,9 +730,13 @@
     grad_in_weight, grad_gain_two = finish_rows(
         functools.partial(in_rows_kernel, seq_size, hidden), in_all, w_in_proj, mlp_gain, seq, (2 * FF,), "in_rows"
     )
+    last_blocks = share_seq(last)
+    grad_normed = sum_blocks(ga_came)
+    grad_inputs = grad_middle + norm_back(grad_normed, gain_one, x)
     if paired():
         kept, sent = halves(down_rows[:, :hidden])
         down_rows = jnp.concatenate(by_core(kept, swap(sent, "fsdp", 1)), axis=0).T
+        down_rows = after(down_rows, grad_in_weight, grad_inputs, last_blocks[1])
         grad_down = jnp.concatenate(in_order(share_seq(down_rows)), axis=1).astype(F32)
     else:
         down = lax.all_gather(down_rows[:, :hidden], ("seq", "fsdp"), axis=0, tiled=True)
@@ -740,9 +744,7 @@
         rows = FF // fsdp_size
         grad_down = lax.dynamic_slice_in_dim(down, fsdp * rows, rows, axis=0).astype(F32)
 
-    grad_normed = sum_blocks(ga_came)
-    grad_inputs = grad_middle + norm_back(grad_normed, gain_one, x)
-    last = after(share_seq(last), grad_in_weight, grad_down, grad_inputs)
+    last = after(last_blocks, grad_in_weight, grad_inputs)
     grad_qkv_weight, grad_out_weight, grad_gain_one = finish_rows(
         functools.partial(last_rows_kernel, seq_size), last, w_qkv, attn_gain, seq, (3 * D, D), "last_rows"
     )

time: 346 us -> 338 us (0.977)
  waiting for transfers between devices: 88.2 us -> 82.8 us
    ppermute x40, waiting for transfers between devices: 83.4 us -> 77.9 us  [swap(): lax.ppermute(x, axis, [(i, i ^ bit) for i in range(lax.axis_size(axis))])]
  transfers between devices with their start and end apart: 48 -> 48, of which waited for: 23 -> 23; matrix products, arithmetic and copies ran while one was open for 16% -> 17% of each run, Pallas kernels for 30% -> 32%
where the time goes in v2:
time: 338 us; the launch traced here: 335 us
  Pallas kernels  111 us (33%)
  waiting for transfers between devices  82.8 us (24%)
  starting transfers between devices  59.1 us (17%)
  other arithmetic  39.3 us (12%)
  local copies, waits for them, and re-layouts  22.8 us (7%)
  between operations  15.3 us (5%)
  matrix products  4.33 us (1%)
    ppermute x40, waiting for transfers between devices, swap(): lax.ppermute(x, axis, [(i, i ^ bit) for i in range(lax.axis_size(axis))])  77.9 us
    ppermute x40, starting transfers between devices, swap(): lax.ppermute(x, axis, [(i, i ^ bit) for i in range(lax.axis_size(axis))])  48.6 us
    pallas_call x4, Pallas kernels, feed_forward(): pl.pallas_call(functools.partial(feed_kernel, hidden), grid_spec=pltpu.Pr...  26.6 us
    pallas_call x1, Pallas kernels, attend_backward(): pl.pallas_call(backward_kernel, grid=(length // rows,), in_specs=[tile, t...  24 us
    pallas_call x1, Pallas kernels, attend_forward(): pl.pallas_call(forward_kernel, grid=(length // rows,), in_specs=[tile, wh...  19 us
    pallas_call x2, Pallas kernels, weight_gradients(): pl.pallas_call(functools.partial(weight_kernel, count, slot, pairs), grid...  13.1 us
    pallas_call x1, Pallas kernels, last_gradients(): pl.pallas_call(last_kernel, grid_spec=pltpu.PrefetchScalarGridSpec(num_sc...  8.15 us
    all_to_all x2, starting transfers between devices, exchange_seq(): lax.all_to_all(blocks, 'seq', split_axis=0, concat_axis=0, tiled=True)  8.07 us
  transfers between devices with their start and end apart: 48, of which 23 were waited for; matrix products, arithmetic and copies ran while one was open for 17% of the time, Pallas kernels for 32%

profile of v2, /device:TPU:0, one launch (start us, length us, event | category | flops | bytes accessed | tf_op | source)
XLA Modules:
  0.0 334.5 jit_solution(1894477071011849818)
XLA Ops:
  12.3 3.1 collective-permute-start.1
  22.7 5.7 %collective-permute-done.1.refs_2_ = bf16[256,1024]{1,0:T(8,128)(2,1)S(1)} collective-permute-done((bf16[256,1024]{1,0:T(8,128)(2,1)}, bf16[256,1024]{1,0:T(8,128)(2,1)S(1)}, u32[]{:S(2)}, u32[]{:S(2)}) %collective-permute-start.1) | collective-permute-done | bytes 524320 | tf_op jit(solution)/shard_map/ppermute | solution.py:23
  28.5 4.2 %collective-permute-start.2 = (bf16[128,1024]{1,0:T(8,128)(2,1)S(1)}, bf16[128,1024]{1,0:T(8,128)(2,1)S(1)}, u32[]{:S(2)}, u32[]{:S(2)}) collective-permute-start(bf16[128,1024]{1,0:T(8,128)(2,1)S(1)} %slice.290), channel_id=1, source_target_pairs={{0,8},{8,0},{16,24},{24,16},{1,9},{9,1},{17,25},{25,17},{2,10},{10... | collective-permute-start | bytes 786440 | tf_op jit(solution)/shard_map/ppermute | solution.py:23
  32.7 4.4 %collective-permute-done.refs_1_ = bf16[256,1024]{1,0:T(8,128)(2,1)} collective-permute-done((bf16[256,1024]{1,0:T(8,128)(2,1)}, bf16[256,1024]{1,0:T(8,128)(2,1)}, u32[]{:S(2)}, u32[]{:S(2)}) %collective-permute-start) | collective-permute-done | bytes 524320 | tf_op jit(solution)/shard_map/ppermute | solution.py:23
  49.9 4.0 %all-gather.3.cloned.1.call-done.refs_4_.w_ref = bf16[1024,1152]{1,0:T(8,128)(2,1)} async-done(((bf16[128,1152]{1,0:T(8,128)(2,1)}), bf16[1024,1152]{1,0:T(8,128)(2,1)}) %all-gather.3.cloned.1.call-update) | async-done | bytes 2359312 | tf_op jit(solution)/shard_map/all_gather | solution.py:63
  58.1 7.2 %qkv.1 = (bf16[1024,1024]{1,0:T(8,128)(2,1)}, bf16[1024,256]{1,0:T(8,128)(2,1)}, bf16[1024,256]{1,0:T(8,128)(2,1)}, bf16[1024,256]{1,0:T(8,128)(2,1)}) custom-call(bf16[256,1024]{1,0:T(8,128)(2,1)} %bitcast.65, bf16[256,1024]{1,0:T(8,128)(2,1)} %collective-permute-done.refs_1_, bf16[256,1024]{1,0:T(8,128)(2,1)} %copy-done.25, bf16[256,1024]{1,0:T(8,128)(2,1)} %copy-done.26, ...), custom_call_target="tpu_custom_call" | custom-call | flops 1610612736 | bytes 7340032 | tf_op jit(solution)/shard_map/qkv/pallas_call | solution.py:140
  71.7 19.0 %attend.1 = (bf16[1024,256]{1,0:T(8,128)(2,1)}, f32[8,1024]{1,0:T(8,128)}) custom-call(bf16[1024,256]{1,0:T(8,128)(2,1)} %get-tuple-element.93.q_ref, bf16[1024,256]{1,0:T(8,128)(2,1)} %get-tuple-element.96.k_ref, bf16[1024,256]{1,0:T(8,128)(2,1)} %get-tuple-element.97.v_ref, s32[1024,1]{1,0:T(8,128)} %copy.39.segc_ref, s32[1024,1]{1,0:T(8,128)} %copy.40.valc_ref, ...), custom_call_target="tpu_custom_call" | custom-call | flops 1073741824 | bytes 2097152 | tf_op jit(solution)/shard_map/attend/pallas_call | solution.py:199
  97.9 6.3 %collective-permute-done.12 = bf16[256,256]{1,0:T(8,128)(2,1)S(1)} collective-permute-done((bf16[256,256]{1,0:T(8,128)(2,1)S(1)}, bf16[256,256]{1,0:T(8,128)(2,1)S(1)}, u32[]{:S(2)}, u32[]{:S(2)}) %collective-permute-start.12) | collective-permute-done | bytes 131104 | tf_op jit(solution)/shard_map/ppermute | solution.py:23
  115.9 6.7 %feed.4 = (bf16[256,656]{1,0:T(8,128)(2,1)}, bf16[256,656]{1,0:T(8,128)(2,1)}, bf16[256,656]{1,0:T(8,128)(2,1)}, f32[256,1024]{1,0:T(8,128)}, bf16[1024,1024]{1,0:T(8,128)(2,1)}) custom-call(s32[1]{0:T(128)} %bitcast.16.me_ref, bf16[256,1024]{1,0:T(8,128)(2,1)} %multiply_convert_fusion.b_ref.refs_0_, bf16[256,1024]{1,0:T(8,128)(2,1)} %bitcast.66, ...), custom_call_target="tpu_custom_call" | custom-call | flops 2063597568 | bytes 7135232 | tf_op jit(solution)/shard_map/feed/pallas_call | solution.py:331
  122.6 4.8 %collective-permute-done.16.b_ref.refs_1_ = bf16[256,1024]{1,0:T(8,128)(2,1)S(1)} collective-permute-done((bf16[256,1024]{1,0:T(8,128)(2,1)}, bf16[256,1024]{1,0:T(8,128)(2,1)S(1)}, u32[]{:S(2)}, u32[]{:S(2)}) %collective-permute-start.16) | collective-permute-done | bytes 524320 | tf_op jit(solution)/shard_map/ppermute | solution.py:23
  128.2 6.6 %feed.5 = (bf16[256,656]{1,0:T(8,128)(2,1)}, bf16[256,656]{1,0:T(8,128)(2,1)}, bf16[256,656]{1,0:T(8,128)(2,1)}, bf16[256,1024]{1,0:T(8,128)(2,1)}, bf16[1024,1024]{1,0:T(8,128)(2,1)}) custom-call(s32[1]{0:T(128)} %bitcast.16.me_ref, bf16[256,1024]{1,0:T(8,128)(2,1)} %copy-done.17, bf16[256,1024]{1,0:T(8,128)(2,1)} %copy-done.5, ...), custom_call_target="tpu_custom_call", output_to_operand_aliasing={{4}: (4, {})} | custom-call | flops 2063597568 | bytes 7135232 | tf_op jit(solution)/shard_map/feed/pallas_call | solution.py:331
  135.8 6.5 %feed.6 = (bf16[256,656]{1,0:T(8,128)(2,1)}, bf16[256,656]{1,0:T(8,128)(2,1)}, bf16[256,656]{1,0:T(8,128)(2,1)}, bf16[256,1024]{1,0:T(8,128)(2,1)}, bf16[1024,1024]{1,0:T(8,128)(2,1)}) custom-call(s32[1]{0:T(128)} %bitcast.16.me_ref, bf16[256,1024]{1,0:T(8,128)(2,1)} %collective-permute-done.20.b_ref.refs_2_, ...), custom_call_target="tpu_custom_call", output_to_operand_aliasing={{4}: (4, {})} | custom-call | flops 2063597568 | bytes 7135232 | tf_op jit(solution)/shard_map/feed/pallas_call | solution.py:331
  142.4 4.5 %collective-permute-done.19 = bf16[256,1024]{1,0:T(8,128)(2,1)S(1)} collective-permute-done((bf16[256,1024]{1,0:T(8,128)(2,1)}, bf16[256,1024]{1,0:T(8,128)(2,1)S(1)}, u32[]{:S(2)}, u32[]{:S(2)}) %collective-permute-start.19) | collective-permute-done | bytes 524320 | tf_op jit(solution)/shard_map/ppermute | solution.py:23
  146.9 6.8 %feed.7 = (bf16[256,656]{1,0:T(8,128)(2,1)}, bf16[256,656]{1,0:T(8,128)(2,1)}, bf16[256,656]{1,0:T(8,128)(2,1)}, bf16[256,1024]{1,0:T(8,128)(2,1)}, bf16[1024,1024]{1,0:T(8,128)(2,1)}) custom-call(s32[1]{0:T(128)} %bitcast.16.me_ref, bf16[256,1024]{1,0:T(8,128)(2,1)} %collective-permute-done.15.b_ref.refs_3_, ...), custom_call_target="tpu_custom_call", output_to_operand_aliasing={{4}: (4, {})} | custom-call | flops 2063597568 | bytes 7135232 | tf_op jit(solution)/shard_map/feed/pallas_call | solution.py:331
  154.5 7.6 %weight_gradients.2.refs_8_ = bf16[1024,2304]{1,0:T(8,128)(2,1)} custom-call(bf16[256,1024]{1,0:T(8,128)(2,1)} %multiply_convert_fusion.b_ref.refs_0_, bf16[256,1024]{1,0:T(8,128)(2,1)} %copy-done.17, bf16[256,1024]{1,0:T(8,128)(2,1)} %collective-permute-done.20.b_ref.refs_2_, bf16[256,1024]{1,0:T(8,128)(2,1)} %collective-permute-done.15.b_ref.refs_3_, ...), custom_call_target="tpu_custom_call" | custom-call | flops 2751463424 | bytes 4784128 | tf_op jit(solution)/shard_map/weight_gradients/pallas_call | solution.py:383
  162.0 3.9 %collective-permute-done.22 = bf16[256,1024]{1,0:T(8,128)(2,1)} collective-permute-done((bf16[256,1024]{1,0:T(8,128)(2,1)}, bf16[256,1024]{1,0:T(8,128)(2,1)}, u32[]{:S(2)}, u32[]{:S(2)}) %collective-permute-start.22) | collective-permute-done | bytes 524320 | tf_op jit(solution)/shard_map/ppermute | solution.py:23
  165.9 5.6 %weight_gradients.3 = bf16[1024,2304]{1,0:T(8,128)(2,1)} custom-call(bf16[256,1024]{1,0:T(8,128)(2,1)} %bitcast.67, bf16[256,1024]{1,0:T(8,128)(2,1)} %copy-done.5, bf16[256,1024]{1,0:T(8,128)(2,1)} %copy-done.4, bf16[256,1024]{1,0:T(8,128)(2,1)} %pad_maximum_fusion.3.g_ref.refs_3_, ...), custom_call_target="tpu_custom_call", output_to_operand_aliasing={{}: (8, {})} | custom-call | flops 1375731712 | bytes 3440640 | tf_op jit(solution)/shard_map/weight_gradients/pallas_call | solution.py:383
  177.5 2.9 collective-permute-start.24
  188.3 4.5 %all-to-all-start = ((bf16[4,256,1024]{2,1,0:T(8,128)(2,1)}), bf16[4,256,1024]{2,1,0:T(8,128)(2,1)}, u32[]{:S(2)}, u32[]{:S(2)}) async-start(bf16[4,256,1024]{2,1,0:T(8,128)(2,1)} %bitcast.18), calls=%async_computation | async-start | bytes 4194304 | tf_op jit(solution)/shard_map/all_to_all | solution.py:47
  192.8 24.0 %attend_back.1.gp_ref = bf16[1024,768]{1,0:T(8,128)(2,1)} custom-call(bf16[1024,256]{1,0:T(8,128)(2,1)} %get-tuple-element.93.q_ref, bf16[1024,256]{1,0:T(8,128)(2,1)} %pad_maximum_fusion.5.go_ref, f32[8,1024]{1,0:T(8,128)} %get-tuple-element.123.lse_ref, bf16[1024,256]{1,0:T(8,128)(2,1)} %get-tuple-element.96.k_ref, ...), custom_call_target="tpu_custom_call" | custom-call | flops 2684354560 | bytes 5242880 | tf_op jit(solution)/shard_map/attend_back/pallas_call | solution.py:266
  216.8 8.1 %last_gradients.1 = (f32[512,768]{1,0:T(8,128)}, bf16[512,768]{1,0:T(8,128)(2,1)}) custom-call(s32[1]{0:T(128)} %bitcast.20.me_ref, bf16[1024,1024]{1,0:T(8,128)(2,1)} %get-tuple-element.122.a_ref, bf16[1024,768]{1,0:T(8,128)(2,1)} %attend_back.1.gp_ref), custom_call_target="tpu_custom_call" | custom-call | flops 1610612736 | bytes 6029312 | tf_op jit(solution)/shard_map/last_gradients/pallas_call | solution.py:415
  224.9 3.6 %fusion.13 = (f32[]{:T(128)}, f32[]{:T(128)}, f32[]{:T(128)}, bf16[1,256,1024]{2,1,0:T(8,128)(2,1)}) fusion(f32[256]{0:T(256)S(1)} %convert_element_type.155, f32[256,1024]{1,0:T(8,128)S(1)} %get-tuple-element.222, bf16[1024,1024]{1,0:T(8,128)(2,1)} %bitcast.19, f32[256,1024]{1,0:T(8,128)S(1)} %get-tuple-element.271), kind=kLoop, calls=%fused_computation.27 | loop fusion | flops 4718589 | bytes 4719628 | tf_op jit(solution)/shard_map/reduce_sum | solution.py:687
  240.4 5.4 %project_back.1 = bf16[1024,1024]{1,0:T(8,128)(2,1)} custom-call(s32[1]{0:T(128)} %bitcast.16.me_ref, bf16[1024,768]{1,0:T(8,128)(2,1)} %attend_back.1.gp_ref, bf16[1024,1152]{1,0:T(8,128)(2,1)} %all-gather.3.cloned.1.call-done.refs_4_.w_ref), custom_call_target="tpu_custom_call" | custom-call | flops 1610612736 | bytes 5242880 | tf_op jit(solution)/shard_map/project_back/pallas_call | solution.py:442
  245.8 2.8 collective-permute-done.32.refs_2_
  250.8 3.6 %all-to-all-start.1 = ((bf16[4,256,1024]{2,1,0:T(8,128)(2,1)}), bf16[4,256,1024]{2,1,0:T(8,128)(2,1)S(1)}, u32[]{:S(2)}, u32[]{:S(2)}) async-start(bf16[4,256,1024]{2,1,0:T(8,128)(2,1)} %bitcast.61), calls=%async_computation.2 | async-start | bytes 4194304 | tf_op jit(solution)/shard_map/all_to_all | solution.py:47
  258.0 3.2 collective-permute-start.30
  264.0 2.9 collective-permute-start.33
  268.6 17.4 %collective-permute-done.29 = bf16[144,768]{1,0:T(8,128)(2,1)} collective-permute-done((bf16[144,768]{1,0:T(8,128)(2,1)S(1)}, bf16[144,768]{1,0:T(8,128)(2,1)}, u32[]{:S(2)}, u32[]{:S(2)}) %collective-permute-start.29) | collective-permute-done | bytes 221216 | tf_op jit(solution)/shard_map/ppermute | solution.py:23
  291.1 3.3 collective-permute-start.37
  297.3 4.1 %in_rows.1 = (f32[128,5248]{1,0:T(8,128)}, f32[1,128]{1,0:T(1,128)}) custom-call(s32[1]{0:T(128)} %bitcast.16.me_ref, bf16[128,1536]{1,0:T(8,128)(2,1)} %slice.243.refs_0_, bf16[128,1536]{1,0:T(8,128)(2,1)} %copy-done.20, bf16[128,1536]{1,0:T(8,128)(2,1)} %copy-done.19, bf16[128,1536]{1,0:T(8,128)(2,1)} %collective-permute-done.33.refs_3_, ...), custom_call_target="tpu_custom_call" | custom-call | bytes 5373952 | tf_op jit(solution)/shard_map/in_rows/pallas_call | solution.py:508
  301.6 13.0 %collective-permute-done.35.refs_1_ = bf16[128,1920]{1,0:T(8,128)(2,1)} collective-permute-done((bf16[128,1920]{1,0:T(8,128)(2,1)S(1)}, bf16[128,1920]{1,0:T(8,128)(2,1)}, u32[]{:S(2)}, u32[]{:S(2)}) %collective-permute-start.35) | collective-permute-done | bytes 491552 | tf_op jit(solution)/shard_map/ppermute | solution.py:23
  321.4 3.3 last_rows.1
  (252 shorter events, 110.2 us)
Async XLA Ops:
  7.2 46.8 %all-gather.3.cloned.1.call-start = ((), (), s32[]{:S(2)}) async-start(), calls=%async_computation.4 | async-start | bytes 2654208 | tf_op jit(solution)/shard_map/all_gather | solution.py:63
  12.3 103.6 %all-gather.5.cloned.1.call-start = ((), (), s32[]{:S(2)}) async-start(), calls=%async_computation.5 | async-start | bytes 5308416 | tf_op jit(solution)/shard_map/all_gather | solution.py:63
  12.3 16.2 %collective-permute-start.1 = (bf16[256,1024]{1,0:T(8,128)(2,1)}, bf16[256,1024]{1,0:T(8,128)(2,1)S(1)}, u32[]{:S(2)}, u32[]{:S(2)}) collective-permute-start(bf16[256,1024]{1,0:T(8,128)(2,1)} %bitcast.63), channel_id=1, source_target_pairs={{0,16},{8,24},{16,0},{24,8},{1,17},{9,25},{17,1},{25,9},{2,18},{10... | collective-permute-start | bytes 1572872 | tf_op jit(solution)/shard_map/ppermute | solution.py:23
  15.4 21.8 %collective-permute-start = (bf16[256,1024]{1,0:T(8,128)(2,1)}, bf16[256,1024]{1,0:T(8,128)(2,1)}, u32[]{:S(2)}, u32[]{:S(2)}) collective-permute-start(bf16[256,1024]{1,0:T(8,128)(2,1)} %bitcast.64), channel_id=1, source_target_pairs={{0,8},{8,0},{16,24},{24,16},{1,9},{9,1},{17,25},{25,17},{2,10},{10... | collective-permute-start | bytes 1572872 | tf_op jit(solution)/shard_map/ppermute | solution.py:23
  17.1 27.5 %collective-permute-start.17 = (bf16[328,256]{0,1:T(8,128)(2,1)S(1)}, bf16[328,256]{0,1:T(8,128)(2,1)S(1)}, u32[]{:S(2)}, u32[]{:S(2)}) collective-permute-start(bf16[328,256]{0,1:T(8,128)(2,1)S(1)} %copy.45), channel_id=1, source_target_pairs={{0,0},{1,1},{2,8},{3,9},{4,16},{5,17},{6,24},{7,25},{8,2},{9,3},{1... | collective-permute-start | bytes 503816 | tf_op jit(solution)/shard_map/ppermute | solution.py:74
  28.5 13.5 %collective-permute-start.2 = (bf16[128,1024]{1,0:T(8,128)(2,1)S(1)}, bf16[128,1024]{1,0:T(8,128)(2,1)S(1)}, u32[]{:S(2)}, u32[]{:S(2)}) collective-permute-start(bf16[128,1024]{1,0:T(8,128)(2,1)S(1)} %slice.290), channel_id=1, source_target_pairs={{0,8},{8,0},{16,24},{24,16},{1,9},{9,1},{17,25},{25,17},{2,10},{10... | collective-permute-start | bytes 786440 | tf_op jit(solution)/shard_map/ppermute | solution.py:23
  47.0 188.1 %reduce-scatter.3.cloned.1.call-start = ((), (), s32[]{:S(2)}) async-start(), calls=%async_computation.6 | async-start | bytes 5308416 | tf_op jit(solution)/shard_map/reduce_scatter | solution.py:670
  47.1 18.2 %collective-permute-start.5 = (bf16[256,1024]{1,0:T(8,128)(2,1)S(1)}, bf16[256,1024]{1,0:T(8,128)(2,1)S(1)}, u32[]{:S(2)}, u32[]{:S(2)}) collective-permute-start(bf16[256,1024]{1,0:T(8,128)(2,1)S(1)} %bitcast.68), channel_id=1, source_target_pairs={{0,16},{8,24},{16,0},{24,8},{1,17},{9,25},{17,1},{25,9},{2,18},{10... | collective-permute-start | bytes 1572872 | tf_op jit(solution)/shard_map/ppermute | solution.py:23
  47.4 17.9 %collective-permute-start.4 = (bf16[256,1024]{1,0:T(8,128)(2,1)S(1)}, bf16[256,1024]{1,0:T(8,128)(2,1)S(1)}, u32[]{:S(2)}, u32[]{:S(2)}) collective-permute-start(bf16[256,1024]{1,0:T(8,128)(2,1)S(1)} %bitcast.69), channel_id=1, source_target_pairs={{0,8},{8,0},{16,24},{24,16},{1,9},{9,1},{17,25},{25,17},{2,10},{10... | collective-permute-start | bytes 1572872 | tf_op jit(solution)/shard_map/ppermute | solution.py:23
  55.8 36.8 %collective-permute-start.7 = (bf16[1024,256]{1,0:T(8,128)(2,1)}, bf16[1024,256]{1,0:T(8,128)(2,1)S(1)}, u32[]{:S(2)}, u32[]{:S(2)}) collective-permute-start(bf16[1024,256]{1,0:T(8,128)(2,1)} %slice.294), channel_id=1, source_target_pairs={{0,16},{8,24},{16,0},{24,8},{1,17},{9,25},{17,1},{25,9},{2,18},{10... | collective-permute-start | bytes 1572872 | tf_op jit(solution)/shard_map/ppermute | solution.py:23
  55.8 36.8 %collective-permute-start.6 = (bf16[1024,256]{1,0:T(8,128)(2,1)}, bf16[1024,256]{1,0:T(8,128)(2,1)S(1)}, u32[]{:S(2)}, u32[]{:S(2)}) collective-permute-start(bf16[1024,256]{1,0:T(8,128)(2,1)} %slice.294), channel_id=1, source_target_pairs={{0,8},{8,0},{16,24},{24,16},{1,9},{9,1},{17,25},{25,17},{2,10},{10... | collective-permute-start | bytes 1572872 | tf_op jit(solution)/shard_map/ppermute | solution.py:23
  65.4 25.4 %collective-permute-start.8 = (bf16[128,1024]{1,0:T(8,128)(2,1)S(1)}, bf16[128,1024]{1,0:T(8,128)(2,1)S(1)}, u32[]{:S(2)}, u32[]{:S(2)}) collective-permute-start(bf16[128,1024]{1,0:T(8,128)(2,1)S(1)} %slice.224), channel_id=1, source_target_pairs={{0,8},{8,0},{16,24},{24,16},{1,9},{9,1},{17,25},{25,17},{2,10},{10... | collective-permute-start | bytes 786440 | tf_op jit(solution)/shard_map/ppermute | solution.py:23
  67.5 23.3 %collective-permute-start.9 = (bf16[128,1024]{1,0:T(8,128)(2,1)S(1)}, bf16[128,1024]{1,0:T(8,128)(2,1)}, u32[]{:S(2)}, u32[]{:S(2)}) collective-permute-start(bf16[128,1024]{1,0:T(8,128)(2,1)S(1)} %slice.225), channel_id=1, source_target_pairs={{0,16},{8,24},{16,0},{24,8},{1,17},{9,25},{17,1},{25,9},{2,18},{10... | collective-permute-start | bytes 786440 | tf_op jit(solution)/shard_map/ppermute | solution.py:23
  92.6 13.8 %collective-permute-start.13 = (bf16[512,256]{1,0:T(8,128)(2,1)S(1)}, bf16[512,256]{1,0:T(8,128)(2,1)S(1)}, u32[]{:S(2)}, u32[]{:S(2)}) collective-permute-start(bf16[512,256]{1,0:T(8,128)(2,1)S(1)} %slice.230), channel_id=1, source_target_pairs={{0,8},{8,0},{16,24},{24,16},{1,9},{9,1},{17,25},{25,17},{2,10},{10... | collective-permute-start | bytes 786440 | tf_op jit(solution)/shard_map/ppermute | solution.py:23
  112.4 15.0 %collective-permute-start.16 = (bf16[256,1024]{1,0:T(8,128)(2,1)}, bf16[256,1024]{1,0:T(8,128)(2,1)S(1)}, u32[]{:S(2)}, u32[]{:S(2)}) collective-permute-start(bf16[256,1024]{1,0:T(8,128)(2,1)} %multiply_convert_fusion.b_ref.refs_0_), channel_id=1, source_target_pairs={{0,8},{8,0},{16,24},{24,16},{1,9},{9,1},{17,25},{25,17},{2,10},{10... | collective-permute-start | bytes 1572872 | tf_op jit(solution)/shard_map/ppermute | solution.py:23
  113.4 22.4 %collective-permute-start.20 = (bf16[256,1024]{1,0:T(8,128)(2,1)}, bf16[256,1024]{1,0:T(8,128)(2,1)}, u32[]{:S(2)}, u32[]{:S(2)}) collective-permute-start(bf16[256,1024]{1,0:T(8,128)(2,1)} %multiply_convert_fusion.b_ref.refs_0_), channel_id=1, source_target_pairs={{0,16},{8,24},{16,0},{24,8},{1,17},{9,25},{17,1},{25,9},{2,18},{10... | collective-permute-start | bytes 1572872 | tf_op jit(solution)/shard_map/ppermute | solution.py:23
  113.5 28.9 %collective-permute-start.15 = (bf16[256,1024]{1,0:T(8,128)(2,1)}, bf16[256,1024]{1,0:T(8,128)(2,1)}, u32[]{:S(2)}, u32[]{:S(2)}) collective-permute-start(bf16[256,1024]{1,0:T(8,128)(2,1)} %multiply_convert_fusion.b_ref.refs_0_), channel_id=1, source_target_pairs={{0,24},{8,16},{16,8},{24,0},{1,25},{9,17},{17,9},{25,1},{2,26},{10... | collective-permute-start | bytes 1572872 | tf_op jit(solution)/shard_map/ppermute | solution.py:23
  134.7 12.2 %collective-permute-start.19 = (bf16[256,1024]{1,0:T(8,128)(2,1)}, bf16[256,1024]{1,0:T(8,128)(2,1)S(1)}, u32[]{:S(2)}, u32[]{:S(2)}) collective-permute-start(bf16[256,1024]{1,0:T(8,128)(2,1)} %get-tuple-element.111), channel_id=1, source_target_pairs={{0,8},{8,0},{16,24},{24,16},{1,9},{9,1},{17,25},{25,17},{2,10},{10... | collective-permute-start | bytes 1572872 | tf_op jit(solution)/shard_map/ppermute | solution.py:23
  142.4 19.7 %collective-permute-start.21 = (bf16[256,1024]{1,0:T(8,128)(2,1)}, bf16[256,1024]{1,0:T(8,128)(2,1)}, u32[]{:S(2)}, u32[]{:S(2)}) collective-permute-start(bf16[256,1024]{1,0:T(8,128)(2,1)} %get-tuple-element.117), channel_id=1, source_target_pairs={{0,16},{8,24},{16,0},{24,8},{1,17},{9,25},{17,1},{25,9},{2,18},{10... | collective-permute-start | bytes 1572872 | tf_op jit(solution)/shard_map/ppermute | solution.py:23
  153.7 12.2 %collective-permute-start.22 = (bf16[256,1024]{1,0:T(8,128)(2,1)}, bf16[256,1024]{1,0:T(8,128)(2,1)}, u32[]{:S(2)}, u32[]{:S(2)}) collective-permute-start(bf16[256,1024]{1,0:T(8,128)(2,1)} %get-tuple-element.118), channel_id=1, source_target_pairs={{0,24},{8,16},{16,8},{24,0},{1,25},{9,17},{17,9},{25,1},{2,26},{10... | collective-permute-start | bytes 1572872 | tf_op jit(solution)/shard_map/ppermute | solution.py:23
  171.5 97.0 %reduce-scatter.5.cloned.1.call-start = ((), (), s32[]{:S(2)}) async-start(), calls=%async_computation.7 | async-start | bytes 2359296 | tf_op jit(solution)/shard_map/reduce_scatter | solution.py:670
  188.3 36.6 %all-to-all-start = ((bf16[4,256,1024]{2,1,0:T(8,128)(2,1)}), bf16[4,256,1024]{2,1,0:T(8,128)(2,1)}, u32[]{:S(2)}, u32[]{:S(2)}) async-start(bf16[4,256,1024]{2,1,0:T(8,128)(2,1)} %bitcast.18), calls=%async_computation | async-start | bytes 4194304 | tf_op jit(solution)/shard_map/all_to_all | solution.py:47
  231.2 23.2 %collective-permute-start.26 = (bf16[512,768]{1,0:T(8,128)(2,1)}, bf16[512,768]{1,0:T(8,128)(2,1)S(1)}, u32[]{:S(2)}, u32[]{:S(2)}) collective-permute-start(bf16[512,768]{1,0:T(8,128)(2,1)} %get-tuple-element.124), channel_id=1, source_target_pairs={{0,1},{1,0},{2,3},{3,2},{4,5},{5,4},{6,7},{7,6},{8,9},{9,8},{10,11... | collective-permute-start | bytes 2359304 | tf_op jit(solution)/shard_map/ppermute | solution.py:23
  236.9 11.7 %collective-permute-start.32 = (bf16[128,1536]{1,0:T(8,128)(2,1)}, bf16[128,1536]{1,0:T(8,128)(2,1)S(1)}, u32[]{:S(2)}, u32[]{:S(2)}) collective-permute-start(bf16[128,1536]{1,0:T(8,128)(2,1)} %slice.243.refs_0_), channel_id=1, source_target_pairs={{0,16},{8,24},{16,0},{24,8},{1,17},{9,25},{17,1},{25,9},{2,18},{10... | collective-permute-start | bytes 1179656 | tf_op jit(solution)/shard_map/ppermute | solution.py:23
  250.8 35.9 %all-to-all-start.1 = ((bf16[4,256,1024]{2,1,0:T(8,128)(2,1)}), bf16[4,256,1024]{2,1,0:T(8,128)(2,1)S(1)}, u32[]{:S(2)}, u32[]{:S(2)}) async-start(bf16[4,256,1024]{2,1,0:T(8,128)(2,1)} %bitcast.61), calls=%async_computation.2 | async-start | bytes 4194304 | tf_op jit(solution)/shard_map/all_to_all | solution.py:47
  261.2 24.7 %collective-permute-start.29 = (bf16[144,768]{1,0:T(8,128)(2,1)S(1)}, bf16[144,768]{1,0:T(8,128)(2,1)}, u32[]{:S(2)}, u32[]{:S(2)}) collective-permute-start(bf16[144,768]{1,0:T(8,128)(2,1)S(1)} %get-tuple-element.264), channel_id=1, source_target_pairs={{0,4},{1,5},{2,6},{3,7},{4,0},{5,1},{6,2},{7,3},{8,12},{9,13},{10,... | collective-permute-start | bytes 663560 | tf_op jit(solution)/shard_map/ppermute | solution.py:23
  261.8 24.2 %collective-permute-start.28 = (bf16[144,768]{1,0:T(8,128)(2,1)S(1)}, bf16[144,768]{1,0:T(8,128)(2,1)}, u32[]{:S(2)}, u32[]{:S(2)}) collective-permute-start(bf16[144,768]{1,0:T(8,128)(2,1)S(1)} %get-tuple-element.265), channel_id=1, source_target_pairs={{0,2},{1,3},{2,0},{3,1},{4,6},{5,7},{6,4},{7,5},{8,10},{9,11},{10,... | collective-permute-start | bytes 663560 | tf_op jit(solution)/shard_map/ppermute | solution.py:23
  264.0 31.2 %collective-permute-start.33 = (bf16[128,1536]{1,0:T(8,128)(2,1)}, bf16[128,1536]{1,0:T(8,128)(2,1)}, u32[]{:S(2)}, u32[]{:S(2)}) collective-permute-start(bf16[128,1536]{1,0:T(8,128)(2,1)} %slice.243.refs_0_), channel_id=1, source_target_pairs={{0,24},{8,16},{16,8},{24,0},{1,25},{9,17},{17,9},{25,1},{2,26},{10... | collective-permute-start | bytes 1179656 | tf_op jit(solution)/shard_map/ppermute | solution.py:23
  266.9 28.2 %collective-permute-start.34 = (bf16[128,768]{1,0:T(8,128)(2,1)}, bf16[128,768]{1,0:T(8,128)(2,1)S(1)}, u32[]{:S(2)}, u32[]{:S(2)}) collective-permute-start(bf16[128,768]{1,0:T(8,128)(2,1)} %slice.244), channel_id=1, source_target_pairs={{0,0},{1,1},{2,8},{3,9},{4,16},{5,17},{6,24},{7,25},{8,2},{9,3},{1... | collective-permute-start | bytes 589832 | tf_op jit(solution)/shard_map/ppermute | solution.py:74
  291.1 27.5 %collective-permute-start.37 = (bf16[128,1920]{1,0:T(8,128)(2,1)S(1)}, bf16[128,1920]{1,0:T(8,128)(2,1)}, u32[]{:S(2)}, u32[]{:S(2)}) collective-permute-start(bf16[128,1920]{1,0:T(8,128)(2,1)S(1)} %pad_maximum_fusion.6.refs_0_), channel_id=1, source_target_pairs={{0,24},{8,16},{16,8},{24,0},{1,25},{9,17},{17,9},{25,1},{2,26},{10... | collective-permute-start | bytes 1474568 | tf_op jit(solution)/shard_map/ppermute | solution.py:23
  294.4 24.2 %collective-permute-start.36 = (bf16[128,1920]{1,0:T(8,128)(2,1)S(1)}, bf16[128,1920]{1,0:T(8,128)(2,1)}, u32[]{:S(2)}, u32[]{:S(2)}) collective-permute-start(bf16[128,1920]{1,0:T(8,128)(2,1)S(1)} %pad_maximum_fusion.6.refs_0_), channel_id=1, source_target_pairs={{0,16},{8,24},{16,0},{24,8},{1,17},{9,25},{17,1},{25,9},{2,18},{10... | collective-permute-start | bytes 1474568 | tf_op jit(solution)/shard_map/ppermute | solution.py:23
  294.4 20.1 %collective-permute-start.35 = (bf16[128,1920]{1,0:T(8,128)(2,1)S(1)}, bf16[128,1920]{1,0:T(8,128)(2,1)}, u32[]{:S(2)}, u32[]{:S(2)}) collective-permute-start(bf16[128,1920]{1,0:T(8,128)(2,1)S(1)} %pad_maximum_fusion.6.refs_0_), channel_id=1, source_target_pairs={{0,8},{8,0},{16,24},{24,16},{1,9},{9,1},{17,25},{25,17},{2,10},{10... | collective-permute-start | bytes 1474568 | tf_op jit(solution)/shard_map/ppermute | solution.py:23
  (49 other events, 394.6 us)
Sparse Core Ops, SparseCore 0:
  12.4 41.5 all-gather.2
  56.2 51.4 all-gather.4
  171.6 56.1 reduce-scatter.2
  230.0 35.1 reduce-scatter.4

commit v3 on v2

--- a/solution.py
+++ b/solution.py
@@ -697,7 +697,7 @@
 
     stats = sum_bit(stats, 1)
     gp_late, stats = after((gp, stats))
-    fed_late, stats = after((fed_rows, stats))
+    fed_late = after(fed_rows, away)
     in_rows, down_rows = fed_late[:, : 2 * slot], fed_late[:, 2 * slot :]
     in_all = share_seq(in_rows)
     ga_parts = project_back(gp_late, first_weight, seq, seq_size)

time: 338 us -> 334 us (0.988)
    unnamed x74 -> x78, local copies, waits for them, and re-layouts: 7.97 us -> 8.8 us
  transfers between devices with their start and end apart: 48 -> 48, of which waited for: 23 -> 19; matrix products, arithmetic and copies ran while one was open for 17% -> 17% of each run, Pallas kernels for 32% -> 32%
where the time goes in v3:
time: 334 us; the launch traced here: 332 us
  Pallas kernels  111 us (33%)
  waiting for transfers between devices  82 us (25%)
  starting transfers between devices  57.6 us (17%)
  other arithmetic  38.4 us (11%)
  local copies, waits for them, and re-layouts  23.5 us (7%)
  between operations  15.2 us (5%)
  matrix products  4.34 us (1%)
    ppermute x40, waiting for transfers between devices, swap(): lax.ppermute(x, axis, [(i, i ^ bit) for i in range(lax.axis_size(axis))])  77.9 us
    ppermute x40, starting transfers between devices, swap(): lax.ppermute(x, axis, [(i, i ^ bit) for i in range(lax.axis_size(axis))])  47.1 us
    pallas_call x4, Pallas kernels, feed_forward(): pl.pallas_call(functools.partial(feed_kernel, hidden), grid_spec=pltpu.Pr...  26.6 us
    pallas_call x1, Pallas kernels, attend_backward(): pl.pallas_call(backward_kernel, grid=(length // rows,), in_specs=[tile, t...  24 us
    pallas_call x1, Pallas kernels, attend_forward(): pl.pallas_call(forward_kernel, grid=(length // rows,), in_specs=[tile, wh...  19 us
    pallas_call x2, Pallas kernels, weight_gradients(): pl.pallas_call(functools.partial(weight_kernel, count, slot, pairs), grid...  13.1 us
    unnamed x78, local copies, waits for them, and re-layouts  8.8 us
    pallas_call x1, Pallas kernels, last_gradients(): pl.pallas_call(last_kernel, grid_spec=pltpu.PrefetchScalarGridSpec(num_sc...  8.15 us
  transfers between devices with their start and end apart: 48, of which 19 were waited for; matrix products, arithmetic and copies ran while one was open for 17% of the time, Pallas kernels for 32%

profile of v3, /device:TPU:0, one launch (start us, length us, event | category | flops | bytes accessed | tf_op | source)
XLA Modules:
  0.0 332.2 jit_solution(4174078344296426992)
XLA Ops:
  12.3 3.1 collective-permute-start.1
  22.7 5.7 %collective-permute-done.1.refs_2_ = bf16[256,1024]{1,0:T(8,128)(2,1)S(1)} collective-permute-done((bf16[256,1024]{1,0:T(8,128)(2,1)}, bf16[256,1024]{1,0:T(8,128)(2,1)S(1)}, u32[]{:S(2)}, u32[]{:S(2)}) %collective-permute-start.1) | collective-permute-done | bytes 524320 | tf_op jit(solution)/shard_map/ppermute | solution.py:23
  28.5 4.2 %collective-permute-start.2 = (bf16[128,1024]{1,0:T(8,128)(2,1)S(1)}, bf16[128,1024]{1,0:T(8,128)(2,1)S(1)}, u32[]{:S(2)}, u32[]{:S(2)}) collective-permute-start(bf16[128,1024]{1,0:T(8,128)(2,1)S(1)} %slice.290), channel_id=1, source_target_pairs={{0,8},{8,0},{16,24},{24,16},{1,9},{9,1},{17,25},{25,17},{2,10},{10... | collective-permute-start | bytes 786440 | tf_op jit(solution)/shard_map/ppermute | solution.py:23
  32.7 4.4 %collective-permute-done.refs_1_ = bf16[256,1024]{1,0:T(8,128)(2,1)} collective-permute-done((bf16[256,1024]{1,0:T(8,128)(2,1)}, bf16[256,1024]{1,0:T(8,128)(2,1)}, u32[]{:S(2)}, u32[]{:S(2)}) %collective-permute-start) | collective-permute-done | bytes 524320 | tf_op jit(solution)/shard_map/ppermute | solution.py:23
  49.9 4.0 %all-gather.3.cloned.1.call-done.refs_4_.w_ref = bf16[1024,1152]{1,0:T(8,128)(2,1)} async-done(((bf16[128,1152]{1,0:T(8,128)(2,1)}), bf16[1024,1152]{1,0:T(8,128)(2,1)}) %all-gather.3.cloned.1.call-update) | async-done | bytes 2359312 | tf_op jit(solution)/shard_map/all_gather | solution.py:63
  58.1 7.2 %qkv.1 = (bf16[1024,1024]{1,0:T(8,128)(2,1)}, bf16[1024,256]{1,0:T(8,128)(2,1)}, bf16[1024,256]{1,0:T(8,128)(2,1)}, bf16[1024,256]{1,0:T(8,128)(2,1)}) custom-call(bf16[256,1024]{1,0:T(8,128)(2,1)} %bitcast.65, bf16[256,1024]{1,0:T(8,128)(2,1)} %collective-permute-done.refs_1_, bf16[256,1024]{1,0:T(8,128)(2,1)} %copy-done.27, bf16[256,1024]{1,0:T(8,128)(2,1)} %copy-done.28, ...), custom_call_target="tpu_custom_call" | custom-call | flops 1610612736 | bytes 7340032 | tf_op jit(solution)/shard_map/qkv/pallas_call | solution.py:140
  71.7 19.0 %attend.1 = (bf16[1024,256]{1,0:T(8,128)(2,1)}, f32[8,1024]{1,0:T(8,128)}) custom-call(bf16[1024,256]{1,0:T(8,128)(2,1)} %get-tuple-element.92.q_ref, bf16[1024,256]{1,0:T(8,128)(2,1)} %get-tuple-element.95.k_ref, bf16[1024,256]{1,0:T(8,128)(2,1)} %get-tuple-element.96.v_ref, s32[1024,1]{1,0:T(8,128)} %copy.39.segc_ref, s32[1024,1]{1,0:T(8,128)} %copy.40.valc_ref, ...), custom_call_target="tpu_custom_call" | custom-call | flops 1073741824 | bytes 2097152 | tf_op jit(solution)/shard_map/attend/pallas_call | solution.py:199
  97.9 6.3 %collective-permute-done.12 = bf16[256,256]{1,0:T(8,128)(2,1)S(1)} collective-permute-done((bf16[256,256]{1,0:T(8,128)(2,1)S(1)}, bf16[256,256]{1,0:T(8,128)(2,1)S(1)}, u32[]{:S(2)}, u32[]{:S(2)}) %collective-permute-start.12) | collective-permute-done | bytes 131104 | tf_op jit(solution)/shard_map/ppermute | solution.py:23
  115.9 6.7 %feed.4 = (bf16[256,656]{1,0:T(8,128)(2,1)}, bf16[256,656]{1,0:T(8,128)(2,1)}, bf16[256,656]{1,0:T(8,128)(2,1)}, f32[256,1024]{1,0:T(8,128)}, bf16[1024,1024]{1,0:T(8,128)(2,1)}) custom-call(s32[1]{0:T(128)} %bitcast.16.me_ref, bf16[256,1024]{1,0:T(8,128)(2,1)} %multiply_convert_fusion.b_ref.refs_0_, bf16[256,1024]{1,0:T(8,128)(2,1)} %bitcast.66, ...), custom_call_target="tpu_custom_call" | custom-call | flops 2063597568 | bytes 7135232 | tf_op jit(solution)/shard_map/feed/pallas_call | solution.py:331
  122.6 4.8 %collective-permute-done.16.b_ref.refs_1_ = bf16[256,1024]{1,0:T(8,128)(2,1)S(1)} collective-permute-done((bf16[256,1024]{1,0:T(8,128)(2,1)}, bf16[256,1024]{1,0:T(8,128)(2,1)S(1)}, u32[]{:S(2)}, u32[]{:S(2)}) %collective-permute-start.16) | collective-permute-done | bytes 524320 | tf_op jit(solution)/shard_map/ppermute | solution.py:23
  128.2 6.6 %feed.5 = (bf16[256,656]{1,0:T(8,128)(2,1)}, bf16[256,656]{1,0:T(8,128)(2,1)}, bf16[256,656]{1,0:T(8,128)(2,1)}, bf16[256,1024]{1,0:T(8,128)(2,1)}, bf16[1024,1024]{1,0:T(8,128)(2,1)}) custom-call(s32[1]{0:T(128)} %bitcast.16.me_ref, bf16[256,1024]{1,0:T(8,128)(2,1)} %copy-done.17, bf16[256,1024]{1,0:T(8,128)(2,1)} %copy-done.5, ...), custom_call_target="tpu_custom_call", output_to_operand_aliasing={{4}: (4, {})} | custom-call | flops 2063597568 | bytes 7135232 | tf_op jit(solution)/shard_map/feed/pallas_call | solution.py:331
  135.8 6.5 %feed.6 = (bf16[256,656]{1,0:T(8,128)(2,1)}, bf16[256,656]{1,0:T(8,128)(2,1)}, bf16[256,656]{1,0:T(8,128)(2,1)}, bf16[256,1024]{1,0:T(8,128)(2,1)}, bf16[1024,1024]{1,0:T(8,128)(2,1)}) custom-call(s32[1]{0:T(128)} %bitcast.16.me_ref, bf16[256,1024]{1,0:T(8,128)(2,1)} %collective-permute-done.20.b_ref.refs_2_, ...), custom_call_target="tpu_custom_call", output_to_operand_aliasing={{4}: (4, {})} | custom-call | flops 2063597568 | bytes 7135232 | tf_op jit(solution)/shard_map/feed/pallas_call | solution.py:331
  142.4 4.5 %collective-permute-done.19 = bf16[256,1024]{1,0:T(8,128)(2,1)S(1)} collective-permute-done((bf16[256,1024]{1,0:T(8,128)(2,1)}, bf16[256,1024]{1,0:T(8,128)(2,1)S(1)}, u32[]{:S(2)}, u32[]{:S(2)}) %collective-permute-start.19) | collective-permute-done | bytes 524320 | tf_op jit(solution)/shard_map/ppermute | solution.py:23
  146.9 6.8 %feed.7 = (bf16[256,656]{1,0:T(8,128)(2,1)}, bf16[256,656]{1,0:T(8,128)(2,1)}, bf16[256,656]{1,0:T(8,128)(2,1)}, bf16[256,1024]{1,0:T(8,128)(2,1)}, bf16[1024,1024]{1,0:T(8,128)(2,1)}) custom-call(s32[1]{0:T(128)} %bitcast.16.me_ref, bf16[256,1024]{1,0:T(8,128)(2,1)} %collective-permute-done.15.b_ref.refs_3_, ...), custom_call_target="tpu_custom_call", output_to_operand_aliasing={{4}: (4, {})} | custom-call | flops 2063597568 | bytes 7135232 | tf_op jit(solution)/shard_map/feed/pallas_call | solution.py:331
  154.5 7.5 %weight_gradients.2.refs_8_ = bf16[1024,2304]{1,0:T(8,128)(2,1)} custom-call(bf16[256,1024]{1,0:T(8,128)(2,1)} %multiply_convert_fusion.b_ref.refs_0_, bf16[256,1024]{1,0:T(8,128)(2,1)} %copy-done.17, bf16[256,1024]{1,0:T(8,128)(2,1)} %collective-permute-done.20.b_ref.refs_2_, bf16[256,1024]{1,0:T(8,128)(2,1)} %collective-permute-done.15.b_ref.refs_3_, ...), custom_call_target="tpu_custom_call" | custom-call | flops 2751463424 | bytes 4784128 | tf_op jit(solution)/shard_map/weight_gradients/pallas_call | solution.py:383
  162.0 3.9 %collective-permute-done.22 = bf16[256,1024]{1,0:T(8,128)(2,1)} collective-permute-done((bf16[256,1024]{1,0:T(8,128)(2,1)}, bf16[256,1024]{1,0:T(8,128)(2,1)}, u32[]{:S(2)}, u32[]{:S(2)}) %collective-permute-start.22) | collective-permute-done | bytes 524320 | tf_op jit(solution)/shard_map/ppermute | solution.py:23
  165.9 5.6 %weight_gradients.3 = bf16[1024,2304]{1,0:T(8,128)(2,1)} custom-call(bf16[256,1024]{1,0:T(8,128)(2,1)} %bitcast.67, bf16[256,1024]{1,0:T(8,128)(2,1)} %copy-done.5, bf16[256,1024]{1,0:T(8,128)(2,1)} %copy-done.4, bf16[256,1024]{1,0:T(8,128)(2,1)} %pad_maximum_fusion.3.g_ref.refs_3_, ...), custom_call_target="tpu_custom_call", output_to_operand_aliasing={{}: (8, {})} | custom-call | flops 1375731712 | bytes 3440640 | tf_op jit(solution)/shard_map/weight_gradients/pallas_call | solution.py:383
  177.5 2.9 collective-permute-start.24
  188.3 4.5 %all-to-all-start = ((bf16[4,256,1024]{2,1,0:T(8,128)(2,1)}), bf16[4,256,1024]{2,1,0:T(8,128)(2,1)}, u32[]{:S(2)}, u32[]{:S(2)}) async-start(bf16[4,256,1024]{2,1,0:T(8,128)(2,1)} %bitcast.18), calls=%async_computation | async-start | bytes 4194304 | tf_op jit(solution)/shard_map/all_to_all | solution.py:47
  192.8 24.0 %attend_back.1.gp_ref = bf16[1024,768]{1,0:T(8,128)(2,1)} custom-call(bf16[1024,256]{1,0:T(8,128)(2,1)} %get-tuple-element.92.q_ref, bf16[1024,256]{1,0:T(8,128)(2,1)} %pad_maximum_fusion.5.go_ref, f32[8,1024]{1,0:T(8,128)} %get-tuple-element.122.lse_ref, bf16[1024,256]{1,0:T(8,128)(2,1)} %get-tuple-element.95.k_ref, ...), custom_call_target="tpu_custom_call" | custom-call | flops 2684354560 | bytes 5242880 | tf_op jit(solution)/shard_map/attend_back/pallas_call | solution.py:266
  216.8 8.2 %last_gradients.1 = (f32[512,768]{1,0:T(8,128)}, bf16[512,768]{1,0:T(8,128)(2,1)}) custom-call(s32[1]{0:T(128)} %bitcast.20.me_ref, bf16[1024,1024]{1,0:T(8,128)(2,1)} %get-tuple-element.121.a_ref, bf16[1024,768]{1,0:T(8,128)(2,1)} %attend_back.1.gp_ref), custom_call_target="tpu_custom_call" | custom-call | flops 1610612736 | bytes 6029312 | tf_op jit(solution)/shard_map/last_gradients/pallas_call | solution.py:415
  225.0 3.6 %fusion.13 = (f32[]{:T(128)}, f32[]{:T(128)}, f32[]{:T(128)}, bf16[1,256,1024]{2,1,0:T(8,128)(2,1)}) fusion(f32[256]{0:T(256)S(1)} %convert_element_type.155, f32[256,1024]{1,0:T(8,128)S(1)} %get-tuple-element.220, bf16[1024,1024]{1,0:T(8,128)(2,1)} %bitcast.19, f32[256,1024]{1,0:T(8,128)S(1)} %get-tuple-element.269), kind=kLoop, calls=%fused_computation.27 | loop fusion | flops 4718589 | bytes 4719628 | tf_op jit(solution)/shard_map/reduce_sum | solution.py:687
  240.3 5.4 %project_back.1 = bf16[1024,1024]{1,0:T(8,128)(2,1)} custom-call(s32[1]{0:T(128)} %bitcast.16.me_ref, bf16[1024,768]{1,0:T(8,128)(2,1)} %attend_back.1.gp_ref, bf16[1024,1152]{1,0:T(8,128)(2,1)} %all-gather.3.cloned.1.call-done.refs_4_.w_ref), custom_call_target="tpu_custom_call" | custom-call | flops 1610612736 | bytes 5242880 | tf_op jit(solution)/shard_map/project_back/pallas_call | solution.py:442
  246.6 3.6 %all-to-all-start.1 = ((bf16[4,256,1024]{2,1,0:T(8,128)(2,1)}), bf16[4,256,1024]{2,1,0:T(8,128)(2,1)S(1)}, u32[]{:S(2)}, u32[]{:S(2)}) async-start(bf16[4,256,1024]{2,1,0:T(8,128)(2,1)} %bitcast.61), calls=%async_computation.2 | async-start | bytes 4194304 | tf_op jit(solution)/shard_map/all_to_all | solution.py:47
  250.2 2.8 fusion.49
  253.1 3.3 collective-permute-start.30
  259.2 2.9 collective-permute-start.33
  263.6 2.8 collective-permute-done.30
  266.4 17.4 %collective-permute-done.29 = bf16[144,768]{1,0:T(8,128)(2,1)S(1)} collective-permute-done((bf16[144,768]{1,0:T(8,128)(2,1)S(1)}, bf16[144,768]{1,0:T(8,128)(2,1)S(1)}, u32[]{:S(2)}, u32[]{:S(2)}) %collective-permute-start.29) | collective-permute-done | bytes 221216 | tf_op jit(solution)/shard_map/ppermute | solution.py:23
  294.6 4.1 %in_rows.1 = (f32[128,5248]{1,0:T(8,128)}, f32[1,128]{1,0:T(1,128)}) custom-call(s32[1]{0:T(128)} %bitcast.16.me_ref, bf16[128,1536]{1,0:T(8,128)(2,1)} %slice.243.refs_0_, bf16[128,1536]{1,0:T(8,128)(2,1)} %copy-done.20, bf16[128,1536]{1,0:T(8,128)(2,1)} %copy-done.19, bf16[128,1536]{1,0:T(8,128)(2,1)} %collective-permute-done.33.refs_3_, ...), custom_call_target="tpu_custom_call" | custom-call | bytes 5373952 | tf_op jit(solution)/shard_map/in_rows/pallas_call | solution.py:508
  298.9 13.4 %collective-permute-done.35.refs_1_ = bf16[128,1920]{1,0:T(8,128)(2,1)} collective-permute-done((bf16[128,1920]{1,0:T(8,128)(2,1)S(1)}, bf16[128,1920]{1,0:T(8,128)(2,1)}, u32[]{:S(2)}, u32[]{:S(2)}) %collective-permute-start.35) | collective-permute-done | bytes 491552 | tf_op jit(solution)/shard_map/ppermute | solution.py:23
  318.4 3.3 %last_rows.1 = (f32[128,3072]{1,0:T(8,128)}, f32[128,1024]{1,0:T(8,128)}, f32[1,128]{1,0:T(1,128)}) custom-call(s32[1]{0:T(128)} %bitcast.16.me_ref, bf16[128,1920]{1,0:T(8,128)(2,1)} %copy-done.8, bf16[128,1920]{1,0:T(8,128)(2,1)} %collective-permute-done.35.refs_1_, bf16[128,1920]{1,0:T(8,128)(2,1)} %collective-permute-done.36.refs_2_, ...), custom_call_target="tpu_custom_call" | custom-call | bytes 4194304 | tf_op jit(solution)/shard_map/last_rows/pallas_call | solution.py:508
  (256 shorter events, 107.9 us)
Async XLA Ops:
  7.2 46.8 %all-gather.3.cloned.1.call-start = ((), (), s32[]{:S(2)}) async-start(), calls=%async_computation.4 | async-start | bytes 2654208 | tf_op jit(solution)/shard_map/all_gather | solution.py:63
  12.3 103.6 %all-gather.5.cloned.1.call-start = ((), (), s32[]{:S(2)}) async-start(), calls=%async_computation.5 | async-start | bytes 5308416 | tf_op jit(solution)/shard_map/all_gather | solution.py:63
  12.3 16.2 %collective-permute-start.1 = (bf16[256,1024]{1,0:T(8,128)(2,1)}, bf16[256,1024]{1,0:T(8,128)(2,1)S(1)}, u32[]{:S(2)}, u32[]{:S(2)}) collective-permute-start(bf16[256,1024]{1,0:T(8,128)(2,1)} %bitcast.63), channel_id=1, source_target_pairs={{0,16},{8,24},{16,0},{24,8},{1,17},{9,25},{17,1},{25,9},{2,18},{10... | collective-permute-start | bytes 1572872 | tf_op jit(solution)/shard_map/ppermute | solution.py:23
  15.4 21.8 %collective-permute-start = (bf16[256,1024]{1,0:T(8,128)(2,1)}, bf16[256,1024]{1,0:T(8,128)(2,1)}, u32[]{:S(2)}, u32[]{:S(2)}) collective-permute-start(bf16[256,1024]{1,0:T(8,128)(2,1)} %bitcast.64), channel_id=1, source_target_pairs={{0,8},{8,0},{16,24},{24,16},{1,9},{9,1},{17,25},{25,17},{2,10},{10... | collective-permute-start | bytes 1572872 | tf_op jit(solution)/shard_map/ppermute | solution.py:23
  17.1 27.5 %collective-permute-start.17 = (bf16[328,256]{0,1:T(8,128)(2,1)S(1)}, bf16[328,256]{0,1:T(8,128)(2,1)S(1)}, u32[]{:S(2)}, u32[]{:S(2)}) collective-permute-start(bf16[328,256]{0,1:T(8,128)(2,1)S(1)} %copy.45), channel_id=1, source_target_pairs={{0,0},{1,1},{2,8},{3,9},{4,16},{5,17},{6,24},{7,25},{8,2},{9,3},{1... | collective-permute-start | bytes 503816 | tf_op jit(solution)/shard_map/ppermute | solution.py:74
  28.5 13.5 %collective-permute-start.2 = (bf16[128,1024]{1,0:T(8,128)(2,1)S(1)}, bf16[128,1024]{1,0:T(8,128)(2,1)S(1)}, u32[]{:S(2)}, u32[]{:S(2)}) collective-permute-start(bf16[128,1024]{1,0:T(8,128)(2,1)S(1)} %slice.290), channel_id=1, source_target_pairs={{0,8},{8,0},{16,24},{24,16},{1,9},{9,1},{17,25},{25,17},{2,10},{10... | collective-permute-start | bytes 786440 | tf_op jit(solution)/shard_map/ppermute | solution.py:23
  47.0 181.5 %reduce-scatter.3.cloned.1.call-start = ((), (), s32[]{:S(2)}) async-start(), calls=%async_computation.6 | async-start | bytes 5308416 | tf_op jit(solution)/shard_map/reduce_scatter | solution.py:670
  47.1 18.2 %collective-permute-start.5 = (bf16[256,1024]{1,0:T(8,128)(2,1)S(1)}, bf16[256,1024]{1,0:T(8,128)(2,1)S(1)}, u32[]{:S(2)}, u32[]{:S(2)}) collective-permute-start(bf16[256,1024]{1,0:T(8,128)(2,1)S(1)} %bitcast.68), channel_id=1, source_target_pairs={{0,16},{8,24},{16,0},{24,8},{1,17},{9,25},{17,1},{25,9},{2,18},{10... | collective-permute-start | bytes 1572872 | tf_op jit(solution)/shard_map/ppermute | solution.py:23
  47.4 17.9 %collective-permute-start.4 = (bf16[256,1024]{1,0:T(8,128)(2,1)S(1)}, bf16[256,1024]{1,0:T(8,128)(2,1)S(1)}, u32[]{:S(2)}, u32[]{:S(2)}) collective-permute-start(bf16[256,1024]{1,0:T(8,128)(2,1)S(1)} %bitcast.69), channel_id=1, source_target_pairs={{0,8},{8,0},{16,24},{24,16},{1,9},{9,1},{17,25},{25,17},{2,10},{10... | collective-permute-start | bytes 1572872 | tf_op jit(solution)/shard_map/ppermute | solution.py:23
  55.8 36.8 %collective-permute-start.7 = (bf16[1024,256]{1,0:T(8,128)(2,1)}, bf16[1024,256]{1,0:T(8,128)(2,1)S(1)}, u32[]{:S(2)}, u32[]{:S(2)}) collective-permute-start(bf16[1024,256]{1,0:T(8,128)(2,1)} %slice.294), channel_id=1, source_target_pairs={{0,16},{8,24},{16,0},{24,8},{1,17},{9,25},{17,1},{25,9},{2,18},{10... | collective-permute-start | bytes 1572872 | tf_op jit(solution)/shard_map/ppermute | solution.py:23
  55.8 36.8 %collective-permute-start.6 = (bf16[1024,256]{1,0:T(8,128)(2,1)}, bf16[1024,256]{1,0:T(8,128)(2,1)S(1)}, u32[]{:S(2)}, u32[]{:S(2)}) collective-permute-start(bf16[1024,256]{1,0:T(8,128)(2,1)} %slice.294), channel_id=1, source_target_pairs={{0,8},{8,0},{16,24},{24,16},{1,9},{9,1},{17,25},{25,17},{2,10},{10... | collective-permute-start | bytes 1572872 | tf_op jit(solution)/shard_map/ppermute | solution.py:23
  65.4 25.4 %collective-permute-start.8 = (bf16[128,1024]{1,0:T(8,128)(2,1)S(1)}, bf16[128,1024]{1,0:T(8,128)(2,1)S(1)}, u32[]{:S(2)}, u32[]{:S(2)}) collective-permute-start(bf16[128,1024]{1,0:T(8,128)(2,1)S(1)} %slice.224), channel_id=1, source_target_pairs={{0,8},{8,0},{16,24},{24,16},{1,9},{9,1},{17,25},{25,17},{2,10},{10... | collective-permute-start | bytes 786440 | tf_op jit(solution)/shard_map/ppermute | solution.py:23
  67.5 23.3 %collective-permute-start.9 = (bf16[128,1024]{1,0:T(8,128)(2,1)S(1)}, bf16[128,1024]{1,0:T(8,128)(2,1)}, u32[]{:S(2)}, u32[]{:S(2)}) collective-permute-start(bf16[128,1024]{1,0:T(8,128)(2,1)S(1)} %slice.225), channel_id=1, source_target_pairs={{0,16},{8,24},{16,0},{24,8},{1,17},{9,25},{17,1},{25,9},{2,18},{10... | collective-permute-start | bytes 786440 | tf_op jit(solution)/shard_map/ppermute | solution.py:23
  92.6 13.8 %collective-permute-start.13 = (bf16[512,256]{1,0:T(8,128)(2,1)S(1)}, bf16[512,256]{1,0:T(8,128)(2,1)S(1)}, u32[]{:S(2)}, u32[]{:S(2)}) collective-permute-start(bf16[512,256]{1,0:T(8,128)(2,1)S(1)} %slice.230), channel_id=1, source_target_pairs={{0,8},{8,0},{16,24},{24,16},{1,9},{9,1},{17,25},{25,17},{2,10},{10... | collective-permute-start | bytes 786440 | tf_op jit(solution)/shard_map/ppermute | solution.py:23
  112.4 15.0 %collective-permute-start.16 = (bf16[256,1024]{1,0:T(8,128)(2,1)}, bf16[256,1024]{1,0:T(8,128)(2,1)S(1)}, u32[]{:S(2)}, u32[]{:S(2)}) collective-permute-start(bf16[256,1024]{1,0:T(8,128)(2,1)} %multiply_convert_fusion.b_ref.refs_0_), channel_id=1, source_target_pairs={{0,8},{8,0},{16,24},{24,16},{1,9},{9,1},{17,25},{25,17},{2,10},{10... | collective-permute-start | bytes 1572872 | tf_op jit(solution)/shard_map/ppermute | solution.py:23
  113.5 22.4 %collective-permute-start.20 = (bf16[256,1024]{1,0:T(8,128)(2,1)}, bf16[256,1024]{1,0:T(8,128)(2,1)}, u32[]{:S(2)}, u32[]{:S(2)}) collective-permute-start(bf16[256,1024]{1,0:T(8,128)(2,1)} %multiply_convert_fusion.b_ref.refs_0_), channel_id=1, source_target_pairs={{0,16},{8,24},{16,0},{24,8},{1,17},{9,25},{17,1},{25,9},{2,18},{10... | collective-permute-start | bytes 1572872 | tf_op jit(solution)/shard_map/ppermute | solution.py:23
  113.5 28.9 %collective-permute-start.15 = (bf16[256,1024]{1,0:T(8,128)(2,1)}, bf16[256,1024]{1,0:T(8,128)(2,1)}, u32[]{:S(2)}, u32[]{:S(2)}) collective-permute-start(bf16[256,1024]{1,0:T(8,128)(2,1)} %multiply_convert_fusion.b_ref.refs_0_), channel_id=1, source_target_pairs={{0,24},{8,16},{16,8},{24,0},{1,25},{9,17},{17,9},{25,1},{2,26},{10... | collective-permute-start | bytes 1572872 | tf_op jit(solution)/shard_map/ppermute | solution.py:23
  142.4 19.7 %collective-permute-start.21 = (bf16[256,1024]{1,0:T(8,128)(2,1)}, bf16[256,1024]{1,0:T(8,128)(2,1)}, u32[]{:S(2)}, u32[]{:S(2)}) collective-permute-start(bf16[256,1024]{1,0:T(8,128)(2,1)} %get-tuple-element.116), channel_id=1, source_target_pairs={{0,16},{8,24},{16,0},{24,8},{1,17},{9,25},{17,1},{25,9},{2,18},{10... | collective-permute-start | bytes 1572872 | tf_op jit(solution)/shard_map/ppermute | solution.py:23
  171.5 113.0 %reduce-scatter.5.cloned.1.call-start = ((), (), s32[]{:S(2)}) async-start(), calls=%async_computation.7 | async-start | bytes 2359296 | tf_op jit(solution)/shard_map/reduce_scatter | solution.py:670
  188.3 36.6 %all-to-all-start = ((bf16[4,256,1024]{2,1,0:T(8,128)(2,1)}), bf16[4,256,1024]{2,1,0:T(8,128)(2,1)}, u32[]{:S(2)}, u32[]{:S(2)}) async-start(bf16[4,256,1024]{2,1,0:T(8,128)(2,1)} %bitcast.18), calls=%async_computation | async-start | bytes 4194304 | tf_op jit(solution)/shard_map/all_to_all | solution.py:47
  225.0 25.2 %collective-permute-start.26 = (bf16[512,768]{1,0:T(8,128)(2,1)}, bf16[512,768]{1,0:T(8,128)(2,1)S(1)}, u32[]{:S(2)}, u32[]{:S(2)}) collective-permute-start(bf16[512,768]{1,0:T(8,128)(2,1)} %get-tuple-element.123), channel_id=1, source_target_pairs={{0,1},{1,0},{2,3},{3,2},{4,5},{5,4},{6,7},{7,6},{8,9},{9,8},{10,11... | collective-permute-start | bytes 2359304 | tf_op jit(solution)/shard_map/ppermute | solution.py:23
  230.3 15.4 %collective-permute-start.32 = (bf16[128,1536]{1,0:T(8,128)(2,1)}, bf16[128,1536]{1,0:T(8,128)(2,1)S(1)}, u32[]{:S(2)}, u32[]{:S(2)}) collective-permute-start(bf16[128,1536]{1,0:T(8,128)(2,1)} %slice.243.refs_0_), channel_id=1, source_target_pairs={{0,16},{8,24},{16,0},{24,8},{1,17},{9,25},{17,1},{25,9},{2,18},{10... | collective-permute-start | bytes 1179656 | tf_op jit(solution)/shard_map/ppermute | solution.py:23
  232.3 13.4 %collective-permute-start.31 = (bf16[128,1536]{1,0:T(8,128)(2,1)}, bf16[128,1536]{1,0:T(8,128)(2,1)S(1)}, u32[]{:S(2)}, u32[]{:S(2)}) collective-permute-start(bf16[128,1536]{1,0:T(8,128)(2,1)} %slice.243.refs_0_), channel_id=1, source_target_pairs={{0,8},{8,0},{16,24},{24,16},{1,9},{9,1},{17,25},{25,17},{2,10},{10... | collective-permute-start | bytes 1179656 | tf_op jit(solution)/shard_map/ppermute | solution.py:23
  246.6 38.0 %all-to-all-start.1 = ((bf16[4,256,1024]{2,1,0:T(8,128)(2,1)}), bf16[4,256,1024]{2,1,0:T(8,128)(2,1)S(1)}, u32[]{:S(2)}, u32[]{:S(2)}) async-start(bf16[4,256,1024]{2,1,0:T(8,128)(2,1)} %bitcast.61), calls=%async_computation.2 | async-start | bytes 4194304 | tf_op jit(solution)/shard_map/all_to_all | solution.py:47
  253.1 13.4 %collective-permute-start.30 = (bf16[144,768]{1,0:T(8,128)(2,1)S(1)}, bf16[144,768]{1,0:T(8,128)(2,1)S(1)}, u32[]{:S(2)}, u32[]{:S(2)}) collective-permute-start(bf16[144,768]{1,0:T(8,128)(2,1)S(1)} %get-tuple-element.261), channel_id=1, source_target_pairs={{0,6},{1,7},{2,4},{3,5},{4,2},{5,3},{6,0},{7,1},{8,14},{9,15},{10,... | collective-permute-start | bytes 663560 | tf_op jit(solution)/shard_map/ppermute | solution.py:23
  256.4 27.4 %collective-permute-start.29 = (bf16[144,768]{1,0:T(8,128)(2,1)S(1)}, bf16[144,768]{1,0:T(8,128)(2,1)S(1)}, u32[]{:S(2)}, u32[]{:S(2)}) collective-permute-start(bf16[144,768]{1,0:T(8,128)(2,1)S(1)} %get-tuple-element.262), channel_id=1, source_target_pairs={{0,4},{1,5},{2,6},{3,7},{4,0},{5,1},{6,2},{7,3},{8,12},{9,13},{10,... | collective-permute-start | bytes 663560 | tf_op jit(solution)/shard_map/ppermute | solution.py:23
  256.9 27.6 %collective-permute-start.28 = (bf16[144,768]{1,0:T(8,128)(2,1)S(1)}, bf16[144,768]{1,0:T(8,128)(2,1)}, u32[]{:S(2)}, u32[]{:S(2)}) collective-permute-start(bf16[144,768]{1,0:T(8,128)(2,1)S(1)} %get-tuple-element.263), channel_id=1, source_target_pairs={{0,2},{1,3},{2,0},{3,1},{4,6},{5,7},{6,4},{7,5},{8,10},{9,11},{10,... | collective-permute-start | bytes 663560 | tf_op jit(solution)/shard_map/ppermute | solution.py:23
  259.2 33.2 %collective-permute-start.33 = (bf16[128,1536]{1,0:T(8,128)(2,1)}, bf16[128,1536]{1,0:T(8,128)(2,1)}, u32[]{:S(2)}, u32[]{:S(2)}) collective-permute-start(bf16[128,1536]{1,0:T(8,128)(2,1)} %slice.243.refs_0_), channel_id=1, source_target_pairs={{0,24},{8,16},{16,8},{24,0},{1,25},{9,17},{17,9},{25,1},{2,26},{10... | collective-permute-start | bytes 1179656 | tf_op jit(solution)/shard_map/ppermute | solution.py:23
  262.1 30.4 %collective-permute-start.34 = (bf16[128,768]{1,0:T(8,128)(2,1)}, bf16[128,768]{1,0:T(8,128)(2,1)S(1)}, u32[]{:S(2)}, u32[]{:S(2)}) collective-permute-start(bf16[128,768]{1,0:T(8,128)(2,1)} %slice.244), channel_id=1, source_target_pairs={{0,0},{1,1},{2,8},{3,9},{4,16},{5,17},{6,24},{7,25},{8,2},{9,3},{1... | collective-permute-start | bytes 589832 | tf_op jit(solution)/shard_map/ppermute | solution.py:74
  288.9 26.9 %collective-permute-start.37 = (bf16[128,1920]{1,0:T(8,128)(2,1)S(1)}, bf16[128,1920]{1,0:T(8,128)(2,1)}, u32[]{:S(2)}, u32[]{:S(2)}) collective-permute-start(bf16[128,1920]{1,0:T(8,128)(2,1)S(1)} %pad_maximum_fusion.6.refs_0_), channel_id=1, source_target_pairs={{0,24},{8,16},{16,8},{24,0},{1,25},{9,17},{17,9},{25,1},{2,26},{10... | collective-permute-start | bytes 1474568 | tf_op jit(solution)/shard_map/ppermute | solution.py:23
  290.2 25.6 %collective-permute-start.36 = (bf16[128,1920]{1,0:T(8,128)(2,1)S(1)}, bf16[128,1920]{1,0:T(8,128)(2,1)}, u32[]{:S(2)}, u32[]{:S(2)}) collective-permute-start(bf16[128,1920]{1,0:T(8,128)(2,1)S(1)} %pad_maximum_fusion.6.refs_0_), channel_id=1, source_target_pairs={{0,16},{8,24},{16,0},{24,8},{1,17},{9,25},{17,1},{25,9},{2,18},{10... | collective-permute-start | bytes 1474568 | tf_op jit(solution)/shard_map/ppermute | solution.py:23
  291.8 20.5 %collective-permute-start.35 = (bf16[128,1920]{1,0:T(8,128)(2,1)S(1)}, bf16[128,1920]{1,0:T(8,128)(2,1)}, u32[]{:S(2)}, u32[]{:S(2)}) collective-permute-start(bf16[128,1920]{1,0:T(8,128)(2,1)S(1)} %pad_maximum_fusion.6.refs_0_), channel_id=1, source_target_pairs={{0,8},{8,0},{16,24},{24,16},{1,9},{9,1},{17,25},{25,17},{2,10},{10... | collective-permute-start | bytes 1474568 | tf_op jit(solution)/shard_map/ppermute | solution.py:23
  (51 other events, 413.9 us)
Sparse Core Ops, SparseCore 0:
  12.4 41.5 all-gather.2
  56.2 51.4 all-gather.4
  171.7 56.1 reduce-scatter.2
  230.1 36.4 reduce-scatter.4
